TPU v7x, 32 devices: a whole 2x2x4 slice. The times are simulated.
32 devices in a mesh: row: 8 (over z, x), col: 4 (over y, core).
Axes of the slice: x: 2, y: 2, z: 4, core: 2. Of those that a mesh axis runs over, the one named last changes fastest.
Arguments:
- patches: bfloat16 [16384, 1024], P('row', 'col'), may hold values from -16 to 16
- w_query: bfloat16 [1024, 1024], P('row', 'col'), may hold values from -0.1875 to 0.1875
- w_key: bfloat16 [1024, 1024], P('row', 'col'), may hold values from -0.1875 to 0.1875
- w_value: bfloat16 [1024, 1024], P('row', 'col'), may hold values from -0.1875 to 0.1875
- w_out: bfloat16 [1024, 1024], P('col', 'row'), may hold values from -2 to 2
- w_gate: bfloat16 [1024, 2816], P('row', 'col'), may hold values from -0.1875 to 0.1875
- w_up: bfloat16 [1024, 2816], P('row', 'col'), may hold values from -0.1875 to 0.1875
- w_down: bfloat16 [2816, 1024], P('col', 'row'), may hold values from -0.109375 to 0.109375
- gain_attn: bfloat16 [1024], P('row'), may hold values from 0.5 to 1.5
- gain_mlp: bfloat16 [1024], P('row'), may hold values from 0.5 to 1.5
- lengths: int32 [16], P('row'), may hold values from 256 to 1024, as said below
- cotangent: bfloat16 [16384, 1024], P('row', 'col'), may hold values from -6 to 6
Outputs:
- output: bfloat16 [16384, 1024], P('row', 'col')
- grad_patches: float32 [16384, 1024], P('row', 'col')
- grad_query: float32 [1024, 1024], P('row', 'col')
- grad_key: float32 [1024, 1024], P('row', 'col')
- grad_value: float32 [1024, 1024], P('row', 'col')
- grad_out: float32 [1024, 1024], P('col', 'row')
- grad_gate: float32 [1024, 2816], P('row', 'col')
- grad_up: float32 [1024, 2816], P('row', 'col')
- grad_down: float32 [2816, 1024], P('col', 'row')
- grad_gain_attn: float32 [1024], P('row')
- grad_gain_mlp: float32 [1024], P('row')
Inputs may be any that keep to these rules, and one draw needn't show every extreme that they name: Each sequence's valid slots are its first lengths[s]; every draw has a sequence with all 1024 slots valid and one with 256.
All inputs are finite; a program needn't handle non-finite values.
Results may differ from a plain program's by a relative error of at most 0.012.
The roundings to bfloat16 on the way count: a program that leaves them out, or rounds other values in their place, can miss the bound.
Values may be sent and summed in bfloat16 or wider, within the bound.
No kernel may reach another device: no remote copies, remote signals or barrier semaphores. Data moves between devices by JAX's collectives and lax.ppermute only.
A program may use at most 192 MiB of HBM per device.

v0:
```python
import jax
import jax.numpy as jnp
from jax import lax
from jax.sharding import PartitionSpec as P

HEAD_DIM = 64


EPSILON = 1e-06
MASKED = -1000000000.0


def times_trans(left, right):
    return lax.dot_general(
        left, right, (((1,), (1,)), ((), ())), preferred_element_type=jnp.float32
    )


def contract_rows(left, right):
    return lax.dot_general(
        left, right, (((0,), (0,)), ((), ())), preferred_element_type=jnp.float32
    )


def shards(
    patches,
    w_query,
    w_key,
    w_value,
    w_out,
    w_gate,
    w_up,
    w_down,
    gain_attn,
    gain_mlp,
    lengths,
    cotangent,
):
    slab = patches.shape[1]
    width = slab * lax.axis_size("col")
    col_start = lax.axis_index("col") * slab
    micro = lengths.shape[0]
    seq = patches.shape[0] // micro
    heads_here = w_query.shape[1] // HEAD_DIM
    scale = HEAD_DIM ** (-0.5)
    block = min(512, seq)
    positions = lax.iota(jnp.int32, seq)

    def fetch():
        return (
            lax.all_gather(w_query, "row", axis=0, tiled=True),
            lax.all_gather(w_key, "row", axis=0, tiled=True),
            lax.all_gather(w_value, "row", axis=0, tiled=True),
            lax.all_gather(w_out, "row", axis=1, tiled=True),
            lax.all_gather(w_gate, "row", axis=0, tiled=True),
            lax.all_gather(w_up, "row", axis=0, tiled=True),
            lax.all_gather(w_down, "row", axis=1, tiled=True),
            lax.all_gather(gain_attn, "row", axis=0, tiled=True),
            lax.all_gather(gain_mlp, "row", axis=0, tiled=True),
        )

    def to_full(values_own):
        return lax.all_gather(values_own, "col", axis=1, tiled=True)

    def reduce_cols(partial_value):
        return lax.psum_scatter(partial_value, "col", scatter_dimension=1, tiled=True)

    def norm_forward(rows_own, gain_whole):
        total = lax.psum(jnp.sum(rows_own * rows_own, axis=1), "col")
        rstd = lax.rsqrt(total / width + EPSILON)
        gain_own = lax.dynamic_slice_in_dim(gain_whole, col_start, slab).astype(jnp.float32)
        normed = (rows_own * rstd[:, None] * gain_own).astype(jnp.bfloat16)
        return (normed, rstd, gain_own)

    def norm_backward(grad_partial, rows_own, rstd, gain_own):
        grad_normed = reduce_cols(grad_partial)
        weighted = grad_normed * gain_own
        gain_piece = jnp.sum(grad_normed * rows_own * rstd[:, None], axis=0)
        gain_whole = lax.dynamic_update_slice_in_dim(
            jnp.zeros((width,), jnp.float32), gain_piece, col_start, 0
        )
        stat, gain_grad = lax.psum((jnp.sum(weighted * rows_own, axis=1), gain_whole), "col")
        grad_rows = (
            rstd[:, None] * weighted - rows_own * (rstd * rstd * rstd * stat / width)[:, None]
        )
        return (grad_rows, gain_grad)

    def split_heads(tensor):
        return jnp.transpose(tensor.reshape(seq, heads_here, HEAD_DIM), (1, 0, 2))

    def join_heads(tensor):
        return jnp.transpose(tensor, (1, 0, 2)).reshape(seq, heads_here * HEAD_DIM)

    def block_scores(query_h, key_h, first_row, last_row, length):
        raw = times_trans(query_h[first_row:last_row], key_h[:last_row]) * scale
        keep = (positions[None, :last_row] <= positions[first_row:last_row, None]) & (
            positions[None, :last_row] < length
        )
        return jnp.where(keep, raw, MASKED)

    outputs = []
    input_grads = []
    totals = None
    for batch in range(micro):
        first_slot = batch * seq
        weights_now = fetch()
        (
            query_full,
            key_full,
            value_full,
            out_full,
            gate_full,
            up_full,
            down_full,
            attn_gain,
            mlp_gain,
        ) = weights_now
        rows_own = patches[first_slot : first_slot + seq].astype(jnp.float32)
        length = lengths[batch]
        valid = (positions < length)[:, None]
        normed_own, rstd_one, gain_one = norm_forward(rows_own, attn_gain)
        normed_one = to_full(normed_own)
        queries = split_heads(
            jnp.dot(normed_one, query_full, preferred_element_type=jnp.float32).astype(jnp.bfloat16)
        )
        keys_all = split_heads(
            jnp.dot(normed_one, key_full, preferred_element_type=jnp.float32).astype(jnp.bfloat16)
        )
        values_all = split_heads(
            jnp.dot(normed_one, value_full, preferred_element_type=jnp.float32).astype(jnp.bfloat16)
        )

        def attend_per_head(operands):
            query_h, key_h, value_h = operands
            pieces = []
            totals = []
            for index in range(seq // block):
                first_row = index * block
                last_row = first_row + block
                scores = block_scores(query_h, key_h, first_row, last_row, length)
                peak = jnp.max(scores, axis=1, keepdims=True)
                expo = jnp.exp(scores - peak)
                denom = jnp.sum(expo, axis=1, keepdims=True)
                probs = (expo / denom).astype(jnp.bfloat16)
                pieces.append(
                    jnp.dot(probs, value_h[:last_row], preferred_element_type=jnp.float32)
                )
                totals.append((peak + jnp.log(denom))[:, 0])
            return (jnp.concatenate(pieces, axis=0), jnp.concatenate(totals, axis=0))

        attended, logsum = lax.map(attend_per_head, (queries, keys_all, values_all))
        attended = join_heads(attended).astype(jnp.bfloat16)
        hstate = rows_own + reduce_cols(
            jnp.dot(attended, out_full, preferred_element_type=jnp.float32)
        )
        normed_own_two, rstd_two, gain_two = norm_forward(hstate, mlp_gain)
        normed_two = to_full(normed_own_two)
        gate = jnp.dot(normed_two, gate_full, preferred_element_type=jnp.float32)
        upward = jnp.dot(normed_two, up_full, preferred_element_type=jnp.float32)
        sigmoid_gate = jax.nn.sigmoid(gate)
        activated = gate * sigmoid_gate
        hidden = (activated * upward).astype(jnp.bfloat16)
        mixed = reduce_cols(jnp.dot(hidden, down_full, preferred_element_type=jnp.float32))
        outputs.append(jnp.where(valid, hstate + mixed, 0.0).astype(jnp.bfloat16))
        weights_back = fetch()
        (
            query_full,
            key_full,
            value_full,
            out_full,
            gate_full,
            up_full,
            down_full,
            attn_gain,
            mlp_gain,
        ) = weights_back
        grad_mixed = jnp.where(
            valid, cotangent[first_slot : first_slot + seq], jnp.zeros((), jnp.bfloat16)
        )
        grad_mixed_full = to_full(grad_mixed)
        grad_hidden = times_trans(grad_mixed_full, down_full)
        down_grad = contract_rows(hidden, grad_mixed_full)
        grad_gate_act = (
            grad_hidden * upward * sigmoid_gate * (1.0 + gate * (1.0 - sigmoid_gate))
        ).astype(jnp.bfloat16)
        grad_up_act = (grad_hidden * activated).astype(jnp.bfloat16)
        gate_grad = contract_rows(normed_two, grad_gate_act)
        up_grad = contract_rows(normed_two, grad_up_act)
        grad_normed_two = times_trans(grad_gate_act, gate_full) + times_trans(grad_up_act, up_full)
        grad_norm_two, mlp_gain_grad = norm_backward(grad_normed_two, hstate, rstd_two, gain_two)
        grad_hstate = grad_mixed.astype(jnp.float32) + grad_norm_two
        grad_branch = to_full(grad_hstate.astype(jnp.bfloat16))
        out_grad = contract_rows(attended, grad_branch)
        grad_attended = split_heads(times_trans(grad_branch, out_full).astype(jnp.bfloat16))

        def per_head(operands):
            query_h, key_h, value_h, grad_h, logsum_h = operands
            query_parts = []
            key_grad = jnp.zeros((seq, HEAD_DIM), jnp.float32)
            value_grad = jnp.zeros((seq, HEAD_DIM), jnp.float32)
            for index in range(seq // block):
                first_row = index * block
                last_row = first_row + block
                scores = block_scores(query_h, key_h, first_row, last_row, length)
                probs = jnp.exp(scores - logsum_h[first_row:last_row, None])
                rounded = probs.astype(jnp.bfloat16)
                grad_probs = times_trans(grad_h[first_row:last_row], value_h[:last_row])
                inner = jnp.sum(probs * grad_probs, axis=1, keepdims=True)
                grad_scores = (probs * (grad_probs - inner)).astype(jnp.bfloat16)
                query_parts.append(
                    jnp.dot(grad_scores, key_h[:last_row], preferred_element_type=jnp.float32)
                    * scale
                )
                key_grad = key_grad.at[:last_row].add(
                    contract_rows(grad_scores, query_h[first_row:last_row]) * scale
                )
                value_grad = value_grad.at[:last_row].add(
                    contract_rows(rounded, grad_h[first_row:last_row])
                )
            query_grad = jnp.concatenate(query_parts, axis=0)
            return (
                query_grad.astype(jnp.bfloat16),
                key_grad.astype(jnp.bfloat16),
                value_grad.astype(jnp.bfloat16),
            )

        grad_queries, grad_keys, grad_values = lax.map(
            per_head, (queries, keys_all, values_all, grad_attended, logsum)
        )
        grad_queries = join_heads(grad_queries)
        grad_keys = join_heads(grad_keys)
        grad_values = join_heads(grad_values)
        query_grad = contract_rows(normed_one, grad_queries)
        key_grad = contract_rows(normed_one, grad_keys)
        value_grad = contract_rows(normed_one, grad_values)
        grad_normed_one = (
            times_trans(grad_queries, query_full)
            + times_trans(grad_keys, key_full)
            + times_trans(grad_values, value_full)
        )
        grad_norm_one, attn_gain_grad = norm_backward(grad_normed_one, rows_own, rstd_one, gain_one)
        input_grads.append(grad_hstate + grad_norm_one)
        local_terms = (
            query_grad,
            key_grad,
            value_grad,
            out_grad,
            gate_grad,
            up_grad,
            down_grad,
            attn_gain_grad,
            mlp_gain_grad,
        )
        reduced = (
            lax.psum_scatter(local_terms[0], "row", scatter_dimension=0, tiled=True),
            lax.psum_scatter(local_terms[1], "row", scatter_dimension=0, tiled=True),
            lax.psum_scatter(local_terms[2], "row", scatter_dimension=0, tiled=True),
            lax.psum_scatter(local_terms[3], "row", scatter_dimension=1, tiled=True),
            lax.psum_scatter(local_terms[4], "row", scatter_dimension=0, tiled=True),
            lax.psum_scatter(local_terms[5], "row", scatter_dimension=0, tiled=True),
            lax.psum_scatter(local_terms[6], "row", scatter_dimension=1, tiled=True),
            lax.psum_scatter(local_terms[7], "row", scatter_dimension=0, tiled=True),
            lax.psum_scatter(local_terms[8], "row", scatter_dimension=0, tiled=True),
        )
        totals = reduced if totals is None else jax.tree.map(jnp.add, totals, reduced)
    return (
        jnp.concatenate(outputs, axis=0),
        jnp.concatenate(input_grads, axis=0),
        totals[0],
        totals[1],
        totals[2],
        totals[3],
        totals[4],
        totals[5],
        totals[6],
        totals[7],
        totals[8],
    )


def solution(mesh):
    placed = (
        P("row", "col"),
        P("row", "col"),
        P("row", "col"),
        P("row", "col"),
        P("col", "row"),
        P("row", "col"),
        P("row", "col"),
        P("col", "row"),
        P("row"),
        P("row"),
        P("row"),
        P("row", "col"),
    )
    return jax.shard_map(
        shards,
        mesh=mesh,
        in_specs=placed,
        out_specs=(
            P("row", "col"),
            P("row", "col"),
            P("row", "col"),
            P("row", "col"),
            P("row", "col"),
            P("col", "row"),
            P("row", "col"),
            P("row", "col"),
            P("col", "row"),
            P("row"),
            P("row"),
        ),
        check_vma=False,
    )
```

profile of v0, /device:TPU:0, one launch (start us, length us, event | category | flops | bytes accessed | tf_op | source)
XLA Modules:
  0.0 1450.2 jit_solution(8379913101905790760)
XLA Ops:
  8.1 22.3 %all-gather = bf16[8,1,128]{2,1,0:T(2,128)(2,1)S(1)} all-gather(bf16[1,1,128]{2,1,0:T(2,128)(2,1)} %bitcast.471), channel_id=1, replica_groups=mesh['row'=8,'col'=4] {'row'}, dimensions={0}, use_global_device_ids=true | all-gather | bytes 2304 | tf_op jit(solution)/shard_map/all_gather | solution.py:58
  41.3 31.7 %all_gather.36 = bf16[1024,256]{1,0:T(8,128)(2,1)S(1)} all-gather(bf16[128,256]{1,0:T(8,128)(2,1)S(1)} %copy-done.36), channel_id=1, replica_groups=mesh['row'=8,'col'=4] {'row'}, dimensions={0}, use_global_device_ids=true | all-gather | bytes 589824 | tf_op jit(solution)/shard_map/all_gather | solution.py:51
  73.0 31.4 %all_gather.37 = bf16[1024,256]{1,0:T(8,128)(2,1)S(1)} all-gather(bf16[128,256]{1,0:T(8,128)(2,1)S(1)} %copy-done.37), channel_id=1, replica_groups=mesh['row'=8,'col'=4] {'row'}, dimensions={0}, use_global_device_ids=true | all-gather | bytes 589824 | tf_op jit(solution)/shard_map/all_gather | solution.py:52
  104.5 33.4 %all_gather.38 = bf16[1024,256]{1,0:T(8,128)(2,1)} all-gather(bf16[128,256]{1,0:T(8,128)(2,1)S(1)} %copy-done.38), channel_id=1, replica_groups=mesh['row'=8,'col'=4] {'row'}, dimensions={0}, use_global_device_ids=true | all-gather | bytes 589824 | tf_op jit(solution)/shard_map/all_gather | solution.py:53
  138.5 28.1 %all_gather.39 = bf16[256,1024]{1,0:T(8,128)(2,1)} all-gather(bf16[256,128]{1,0:T(8,128)(2,1)S(1)} %copy-done.39), channel_id=1, replica_groups=mesh['row'=8,'col'=4] {'row'}, dimensions={1}, use_global_device_ids=true | all-gather | bytes 589824 | tf_op jit(solution)/shard_map/all_gather | solution.py:54
  179.1 34.7 %while.74 = (s32[]{:T(128)}, bf16[4,1024,64]{1,2,0:T(8,128)(2,1)}, f32[4,1024]{1,0:T(4,128)S(1)}, s32[1024]{0:T(1024)S(1)}, s32[]{:T(128)}, /*index=5*/bf16[4,10...) while((s32[]{:T(128)}, bf16[4,1024,64]{1,2,0:T(8,128)(2,1)}, ...), condition=%wide.region_7.8_spmd.clone, body=%wide.region_2.7_spmd.clone.sunk | while | flops 209454592 | bytes 10959497 | solution.py:151
  231.3 34.8 %while.75 = (s32[]{:T(128)}, bf16[4,1024,64]{1,2,0:T(8,128)(2,1)}, f32[4,1024]{1,0:T(4,128)S(1)}, s32[1024]{0:T(1024)S(1)}, s32[]{:T(128)}, /*index=5*/bf16[4,10...) while((s32[]{:T(128)}, bf16[4,1024,64]{1,2,0:T(8,128)(2,1)}, ...), condition=%wide.region_19.20_spmd.clone, body=%wide.region_14.19_spmd.clone.sunk | while | flops 209454592 | bytes 10959497 | solution.py:151
  270.7 16.3 %all-gather.1 = bf16[8,1,128]{2,1,0:T(2,128)(2,1)S(1)} all-gather(bf16[1,1,128]{2,1,0:T(2,128)(2,1)S(1)} %bitcast.472), channel_id=1, replica_groups=mesh['row'=8,'col'=4] {'row'}, dimensions={0}, use_global_device_ids=true | all-gather | bytes 2304 | tf_op jit(solution)/shard_map/all_gather | solution.py:59
  287.1 25.6 %reduce-scatter.20.cloned.1.call-done = f32[1024,256]{1,0:T(8,128)} async-done(((f32[1024,1024]{1,0:T(8,128)}), f32[1024,256]{1,0:T(8,128)}) %reduce-scatter.20.cloned.1.call-update) | async-done | bytes 1048592 | tf_op jit(solution)/shard_map/reduce_scatter | solution.py:66
  326.3 19.3 %all-gather.16.cloned.1.call-done = bf16[1024,1024]{1,0:T(8,128)(2,1)} async-done(((bf16[1024,256]{1,0:T(8,128)(2,1)}), bf16[1024,1024]{1,0:T(8,128)(2,1)}) %all-gather.16.cloned.1.call-update) | async-done | bytes 2097168 | tf_op jit(solution)/shard_map/all_gather | solution.py:63
  350.8 39.8 %all-gather.20.cloned.1.call-done = bf16[1024,704]{0,1:T(8,128)(2,1)} async-done(((bf16[128,704]{0,1:T(8,128)(2,1)}), bf16[1024,704]{0,1:T(8,128)(2,1)}) %all-gather.20.cloned.1.call-update) | async-done | bytes 1441808 | tf_op jit(solution)/shard_map/all_gather | solution.py:56
  395.9 38.2 %all-gather.22.cloned.1.call-done = bf16[704,1024]{1,0:T(8,128)(2,1)} async-done(((bf16[704,128]{1,0:T(8,128)(2,1)}), bf16[704,1024]{1,0:T(8,128)(2,1)}) %all-gather.22.cloned.1.call-update) | async-done | bytes 1441808 | tf_op jit(solution)/shard_map/all_gather | solution.py:57
  434.1 22.5 %all-gather.28.cloned.1.call-done = bf16[1024,1024]{1,0:T(8,128)(2,1)} async-done(((bf16[1024,256]{1,0:T(8,128)(2,1)}), bf16[1024,1024]{1,0:T(8,128)(2,1)}) %all-gather.28.cloned.1.call-update) | async-done | bytes 2097168 | tf_op jit(solution)/shard_map/all_gather | solution.py:63
  456.6 7.6 multiply_convert_fusion.6
  470.7 44.5 %reduce-scatter.24.cloned.1.call-done = f32[1024,256]{1,0:T(8,128)} async-done(((f32[1024,1024]{1,0:T(8,128)}), f32[1024,256]{1,0:T(8,128)}) %reduce-scatter.24.cloned.1.call-update) | async-done | bytes 1048592 | tf_op jit(solution)/shard_map/reduce_scatter | solution.py:66
  519.2 21.7 %all-gather.26.cloned.1.call-done = bf16[1024,1024]{1,0:T(8,128)(2,1)} async-done(((bf16[1024,256]{1,0:T(8,128)(2,1)}), bf16[1024,1024]{1,0:T(8,128)(2,1)}) %all-gather.26.cloned.1.call-update) | async-done | bytes 2097168 | tf_op jit(solution)/shard_map/all_gather | solution.py:63
  549.6 15.5 %all-gather.32.cloned.1.call-done = bf16[1024,1024]{1,0:T(8,128)(2,1)} async-done(((bf16[1024,256]{1,0:T(8,128)(2,1)}), bf16[1024,1024]{1,0:T(8,128)(2,1)}) %all-gather.32.cloned.1.call-update) | async-done | bytes 2097168 | tf_op jit(solution)/shard_map/all_gather | solution.py:63
  565.1 7.7 multiply_convert_fusion.4
  579.2 44.6 %reduce-scatter.28.cloned.1.call-done = f32[1024,256]{1,0:T(8,128)} async-done(((f32[1024,1024]{1,0:T(8,128)}), f32[1024,256]{1,0:T(8,128)}) %reduce-scatter.28.cloned.1.call-update) | async-done | bytes 1048592 | tf_op jit(solution)/shard_map/reduce_scatter | solution.py:66
  635.3 22.9 %all-gather.30.cloned.1.call-done = bf16[1024,1024]{1,0:T(8,128)(2,1)} async-done(((bf16[1024,256]{1,0:T(8,128)(2,1)}), bf16[1024,1024]{1,0:T(8,128)(2,1)}) %all-gather.30.cloned.1.call-update) | async-done | bytes 2097168 | tf_op jit(solution)/shard_map/all_gather | solution.py:63
  663.8 63.1 %while.76 = (s32[]{:T(128)}, bf16[4,1024,64]{1,2,0:T(8,128)(2,1)}, bf16[4,1024,64]{1,2,0:T(8,128)(2,1)}, bf16[4,1024,64]{1,2,0:T(8,128)(2,1)}, s32[1024]{0:T(102...) while((s32[]{:T(128)}, bf16[4,1024,64]{1,2,0:T(8,128)(2,1)}, ...), condition=%wide.region_30.31_spmd.clone, body=%wide.region_27.30_spmd.clone.sunk | while | flops 512721408 | bytes 27057332 | solution.py:227
  739.8 63.3 %while.77 = (s32[]{:T(128)}, bf16[4,1024,64]{1,2,0:T(8,128)(2,1)}, bf16[4,1024,64]{1,2,0:T(8,128)(2,1)}, bf16[4,1024,64]{1,2,0:T(8,128)(2,1)}, s32[1024]{0:T(102...) while((s32[]{:T(128)}, bf16[4,1024,64]{1,2,0:T(8,128)(2,1)}, ...), condition=%wide.region_40.41_spmd.clone, body=%wide.region_37.40_spmd.clone.sunk | while | flops 512721408 | bytes 27057332 | solution.py:227
  866.6 21.1 %all-reduce.6 = (f32[1024]{0:T(1024)S(1)}, f32[1024]{0:T(1024)S(1)}) all-reduce(f32[1024]{0:T(1024)S(1)} %add_dynamic-update-slice_fusion.1, f32[1024]{0:T(1024)S(1)} %add_dynamic-update-slice_fusion), channel_id=26, replica_groups=mesh['row'=8,'col'=4] {'row'}, use_global_device_ids=true, to_apply=%region_60.61.clone | all-reduce | flops 2048 | bytes 16384
  887.9 7.3 all-reduce.7
  904.6 43.9 %reduce-scatter.22.cloned.1.call-done = f32[1024,256]{1,0:T(8,128)} async-done(((f32[1024,1024]{1,0:T(8,128)}), f32[1024,256]{1,0:T(8,128)}) %reduce-scatter.22.cloned.1.call-update) | async-done | bytes 1048592 | tf_op jit(solution)/shard_map/reduce_scatter | solution.py:66
  954.1 70.7 %reduce-scatter.42.cloned.1.call-done = f32[128,704]{0,1:T(8,128)} async-done(((f32[1024,704]{0,1:T(8,128)}), f32[128,704]{0,1:T(8,128)}) %reduce-scatter.42.cloned.1.call-update) | async-done | bytes 360464 | tf_op jit(solution)/shard_map/reduce_scatter | solution.py:260
  1024.8 75.6 %reduce-scatter.40.cloned.1.call-done = f32[128,704]{0,1:T(8,128)} async-done(((f32[1024,704]{0,1:T(8,128)}), f32[128,704]{0,1:T(8,128)}) %reduce-scatter.40.cloned.1.call-update) | async-done | bytes 360464 | tf_op jit(solution)/shard_map/reduce_scatter | solution.py:259
  1100.4 75.4 %reduce-scatter.44.cloned.1.call-done = f32[704,128]{1,0:T(8,128)} async-done(((f32[704,1024]{1,0:T(8,128)}), f32[704,128]{1,0:T(8,128)}) %reduce-scatter.44.cloned.1.call-update) | async-done | bytes 360464 | tf_op jit(solution)/shard_map/reduce_scatter | solution.py:261
  1175.8 67.1 %reduce-scatter.38.cloned.1.call-done = f32[256,128]{1,0:T(8,128)} async-done(((f32[256,1024]{1,0:T(8,128)}), f32[256,128]{1,0:T(8,128)}) %reduce-scatter.38.cloned.1.call-update) | async-done | bytes 131088 | tf_op jit(solution)/shard_map/reduce_scatter | solution.py:258
  1242.9 66.7 %reduce-scatter.36.cloned.1.call-done = f32[128,256]{1,0:T(8,128)} async-done(((f32[1024,256]{1,0:T(8,128)}), f32[128,256]{1,0:T(8,128)}) %reduce-scatter.36.cloned.1.call-update) | async-done | bytes 131088 | tf_op jit(solution)/shard_map/reduce_scatter | solution.py:257
  1309.6 66.2 %reduce-scatter.34.cloned.1.call-done = f32[128,256]{1,0:T(8,128)} async-done(((f32[1024,256]{1,0:T(8,128)}), f32[128,256]{1,0:T(8,128)}) %reduce-scatter.34.cloned.1.call-update) | async-done | bytes 131088 | tf_op jit(solution)/shard_map/reduce_scatter | solution.py:256
  1375.8 66.7 %reduce-scatter.32.cloned.1.call-done = f32[128,256]{1,0:T(8,128)} async-done(((f32[1024,256]{1,0:T(8,128)}), f32[128,256]{1,0:T(8,128)}) %reduce-scatter.32.cloned.1.call-update) | async-done | bytes 131088 | tf_op jit(solution)/shard_map/reduce_scatter | solution.py:255
  (554 shorter events, 397.6 us)
Async XLA Ops:
  8.0 158.5 %all-gather.14.cloned.1.call-start = ((), (), s32[]{:S(2)}) async-start(), calls=%async_computation.15 | async-start | bytes 2621440 | tf_op jit(solution)/shard_map/all_gather | solution.py:63
  37.9 66.6 %copy-start.38 = (bf16[128,256]{1,0:T(8,128)(2,1)S(1)}, bf16[128,256]{1,0:T(8,128)(2,1)}, u32[]{:S(2)}) copy-start(bf16[128,256]{1,0:T(8,128)(2,1)} %param.47) | copy-start | bytes 196612
  37.9 100.0 %copy-start.55 = (s32[2]{0:T(128)S(1)}, s32[2]{0:T(128)}, u32[]{:S(2)}) copy-start(s32[2]{0:T(128)} %param.54) | copy-start | bytes 28
  37.9 100.6 %copy-start.39 = (bf16[256,128]{1,0:T(8,128)(2,1)S(1)}, bf16[256,128]{1,0:T(8,128)(2,1)}, u32[]{:S(2)}) copy-start(bf16[256,128]{1,0:T(8,128)(2,1)} %param.48) | copy-start | bytes 196612
  40.5 177.6 %all-gather.24.cloned.1.call-start = ((), (), s32[]{:S(2)}) async-start(), calls=%async_computation.22 | async-start | bytes 2621440 | tf_op jit(solution)/shard_map/all_gather | solution.py:63
  41.2 245.8 %reduce-scatter.16.cloned.1.call-start = ((), (), s32[]{:S(2)}) async-start(), calls=%async_computation.16 | async-start | bytes 5242880 | tf_op jit(solution)/shard_map/reduce_scatter | solution.py:66
  73.0 96.8 %copy-start.13 = (bf16[1024,256]{1,0:T(8,128)(2,1)}, bf16[1024,256]{1,0:T(8,128)(2,1)S(1)}, u32[]{:S(2)}) copy-start(bf16[1024,256]{1,0:T(8,128)(2,1)S(1)} %all_gather.36) | copy-start | bytes 1572868
  104.5 67.7 %copy-start.17 = (bf16[1024,256]{1,0:T(8,128)(2,1)}, bf16[1024,256]{1,0:T(8,128)(2,1)S(1)}, u32[]{:S(2)}) copy-start(bf16[1024,256]{1,0:T(8,128)(2,1)S(1)} %all_gather.37) | copy-start | bytes 1572868
  217.8 94.9 %reduce-scatter.20.cloned.1.call-start = ((), (), s32[]{:S(2)}) async-start(), calls=%async_computation.23 | async-start | bytes 5242880 | tf_op jit(solution)/shard_map/reduce_scatter | solution.py:66
  270.1 56.2 %all-gather.18.cloned.1.call-start = ((), (), s32[]{:S(2)}) async-start(), calls=%async_computation.18 | async-start | bytes 1622016 | tf_op jit(solution)/shard_map/all_gather | solution.py:55
  270.6 75.0 %all-gather.16.cloned.1.call-start = ((), (), s32[]{:S(2)}) async-start(), calls=%async_computation.17 | async-start | bytes 2621440 | tf_op jit(solution)/shard_map/all_gather | solution.py:63
  314.6 316.8 %copy-start.8 = (f32[1024,256]{1,0:T(8,128)}, f32[1024,256]{1,0:T(8,128)S(1)}, u32[]{:S(2)}) copy-start(f32[1024,256]{1,0:T(8,128)S(1)} %get-tuple-element.830) | copy-start | bytes 3145732
  321.7 69.0 %all-gather.20.cloned.1.call-start = ((), (), s32[]{:S(2)}) async-start(), calls=%async_computation.19 | async-start | bytes 1622016 | tf_op jit(solution)/shard_map/all_gather | solution.py:56
  322.2 111.9 %all-gather.22.cloned.1.call-start = ((), (), s32[]{:S(2)}) async-start(), calls=%async_computation.20 | async-start | bytes 1622016 | tf_op jit(solution)/shard_map/all_gather | solution.py:57
  323.0 133.6 %all-gather.28.cloned.1.call-start = ((), (), s32[]{:S(2)}) async-start(), calls=%async_computation.26 | async-start | bytes 2621440 | tf_op jit(solution)/shard_map/all_gather | solution.py:63
  325.9 189.2 %reduce-scatter.24.cloned.1.call-start = ((), (), s32[]{:S(2)}) async-start(), calls=%async_computation.27 | async-start | bytes 5242880 | tf_op jit(solution)/shard_map/reduce_scatter | solution.py:66
  470.6 70.3 %all-gather.26.cloned.1.call-start = ((), (), s32[]{:S(2)}) async-start(), calls=%async_computation.24 | async-start | bytes 2621440 | tf_op jit(solution)/shard_map/all_gather | solution.py:63
  518.1 47.0 %all-gather.32.cloned.1.call-start = ((), (), s32[]{:S(2)}) async-start(), calls=%async_computation.30 | async-start | bytes 2621440 | tf_op jit(solution)/shard_map/all_gather | solution.py:63
  518.7 105.1 %reduce-scatter.28.cloned.1.call-start = ((), (), s32[]{:S(2)}) async-start(), calls=%async_computation.31 | async-start | bytes 5242880 | tf_op jit(solution)/shard_map/reduce_scatter | solution.py:66
  579.1 79.2 %all-gather.30.cloned.1.call-start = ((), (), s32[]{:S(2)}) async-start(), calls=%async_computation.28 | async-start | bytes 2621440 | tf_op jit(solution)/shard_map/all_gather | solution.py:63
  634.4 92.5 %all-gather.34.cloned.1.call-start = ((), (), s32[]{:S(2)}) async-start(), calls=%async_computation.32 | async-start | bytes 2621440 | tf_op jit(solution)/shard_map/all_gather | solution.py:63
  635.1 227.9 %reduce-scatter.26.cloned.1.call-start = ((), (), s32[]{:S(2)}) async-start(), calls=%async_computation.29 | async-start | bytes 5242880 | tf_op jit(solution)/shard_map/reduce_scatter | solution.py:66
  737.0 126.1 %reduce-scatter.30.cloned.1.call-start = ((), (), s32[]{:S(2)}) async-start(), calls=%async_computation.33 | async-start | bytes 5242880 | tf_op jit(solution)/shard_map/reduce_scatter | solution.py:66
  809.2 92.0 %reduce-scatter.18.cloned.1.call-start = ((), (), s32[]{:S(2)}) async-start(), calls=%async_computation.21 | async-start | bytes 5242880 | tf_op jit(solution)/shard_map/reduce_scatter | solution.py:66
  815.8 132.7 %reduce-scatter.22.cloned.1.call-start = ((), (), s32[]{:S(2)}) async-start(), calls=%async_computation.25 | async-start | bytes 5242880 | tf_op jit(solution)/shard_map/reduce_scatter | solution.py:66
  821.2 203.6 %reduce-scatter.42.cloned.1.call-start = ((), (), s32[]{:S(2)}) async-start(), calls=%async_computation.39 | async-start | bytes 3244032 | tf_op jit(solution)/shard_map/reduce_scatter | solution.py:260
  829.2 271.2 %reduce-scatter.40.cloned.1.call-start = ((), (), s32[]{:S(2)}) async-start(), calls=%async_computation.38 | async-start | bytes 3244032 | tf_op jit(solution)/shard_map/reduce_scatter | solution.py:259
  836.0 339.7 %reduce-scatter.44.cloned.1.call-start = ((), (), s32[]{:S(2)}) async-start(), calls=%async_computation.40 | async-start | bytes 3244032 | tf_op jit(solution)/shard_map/reduce_scatter | solution.py:261
  844.2 398.7 %reduce-scatter.38.cloned.1.call-start = ((), (), s32[]{:S(2)}) async-start(), calls=%async_computation.37 | async-start | bytes 1179648 | tf_op jit(solution)/shard_map/reduce_scatter | solution.py:258
  849.4 460.2 %reduce-scatter.36.cloned.1.call-start = ((), (), s32[]{:S(2)}) async-start(), calls=%async_computation.36 | async-start | bytes 1179648 | tf_op jit(solution)/shard_map/reduce_scatter | solution.py:257
  853.3 522.6 %reduce-scatter.34.cloned.1.call-start = ((), (), s32[]{:S(2)}) async-start(), calls=%async_computation.35 | async-start | bytes 1179648 | tf_op jit(solution)/shard_map/reduce_scatter | solution.py:256
  857.2 585.4 %reduce-scatter.32.cloned.1.call-start = ((), (), s32[]{:S(2)}) async-start(), calls=%async_computation.34 | async-start | bytes 1179648 | tf_op jit(solution)/shard_map/reduce_scatter | solution.py:255
  (71 other events, 573.1 us)
Sparse Core Ops, SparseCore 0:
  40.6 20.3 all-gather.13
  63.1 22.8 all-gather.23
  217.9 42.5 reduce-scatter.15
  270.2 42.4 reduce-scatter.19
  579.3 44.5 reduce-scatter.27
  737.1 44.5 reduce-scatter.25
  809.3 44.3 reduce-scatter.29
  856.3 44.9 reduce-scatter.17
  903.9 44.5 reduce-scatter.21
  952.5 72.3 reduce-scatter.41
  1029.0 71.4 reduce-scatter.39
  1104.4 71.3 reduce-scatter.43
  1179.7 63.1 reduce-scatter.37
  1247.1 62.4 reduce-scatter.35
  1313.5 62.3 reduce-scatter.33
  1380.0 62.4 reduce-scatter.31
Sparse Core Ops, SparseCore 1:
  272.6 41.1 all-gather.17
  321.7 23.8 all-gather.15
  347.5 43.1 all-gather.19
  392.7 41.3 all-gather.21
  435.7 20.9 all-gather.27
  470.7 44.4 reduce-scatter.23
  518.2 22.6 all-gather.25
  542.4 22.7 all-gather.31
  634.5 23.8 all-gather.29
  659.9 22.7 all-gather.33
where the time goes:
time: 1460 us; the launch traced here: 1450 us
  waiting for transfers between devices  837 us (57%)
  matrix products  278 us (19%)
  blocking collectives  209 us (14%)
  other arithmetic  71 us (5%)
  local copies, waits for them, and re-layouts  33.4 us (2%)
  between operations  17.7 us (1%)
    reduce_scatter x8, waiting for transfers between devices, reduce_cols(): lax.psum_scatter(partial_value, 'col', scatter_dimension=1, tiled=True)  165 us
    dot_general x62, matrix products, times_trans(): lax.dot_general(left, right, (((1,), (1,)), ((), ())), preferred_element_...  117 us
    all_gather x8, waiting for transfers between devices, to_full(): return lax.all_gather(values_own, 'col', axis=1, tiled=True)  102 us
    reduce_scatter x1, waiting for transfers between devices, shards(): lax.psum_scatter(local_terms[4], 'row', scatter_dimension=0, tiled=True)  75.6 us
    reduce_scatter x1, waiting for transfers between devices, shards(): lax.psum_scatter(local_terms[6], 'row', scatter_dimension=1, tiled=True)  75.4 us
    reduce_scatter x1, waiting for transfers between devices, shards(): lax.psum_scatter(local_terms[5], 'row', scatter_dimension=0, tiled=True)  70.7 us
    dot_general x46, matrix products, contract_rows(): lax.dot_general(left, right, (((0,), (0,)), ((), ())), preferred_element_...  69.9 us
    reduce_scatter x1, waiting for transfers between devices, shards(): lax.psum_scatter(local_terms[3], 'row', scatter_dimension=1, tiled=True)  67.1 us
  transfers between devices with their start and end apart: 26, of which 19 were waited for; matrix products, arithmetic and copies ran while one was open for 22% of the time, Pallas kernels for 0%

commit v1 on v0

v1 whole, which is shorter than its diff:
```python
import functools

import jax
import jax.numpy as jnp
from jax import lax
from jax.experimental import pallas as pl
from jax.experimental.pallas import tpu as pltpu
from jax.sharding import PartitionSpec as P

HEAD_DIM = 64
PAIR = 2 * HEAD_DIM
EPSILON = 1e-06
MASKED = -1000000000.0
BF16 = jnp.bfloat16
F32 = jnp.float32
MIB = 1 << 20

NN = (((1,), (0,)), ((), ()))
NT = (((1,), (1,)), ((), ()))
TN = (((0,), (0,)), ((), ()))

ANY = pl.BlockSpec(memory_space=pl.ANY)
SCALARS = pl.BlockSpec(memory_space=pltpu.SMEM)


def mm(left, right, dims):
    return lax.dot_general(left, right, dims, preferred_element_type=F32)


def params(mib):
    return pltpu.CompilerParams(
        dimension_semantics=("arbitrary",), vmem_limit_bytes=mib * MIB
    )


def fetch_copies(me, buffers, first, scratch, sems):
    zs, rows, _ = buffers[0].shape
    out = []
    for at, buffer in enumerate(buffers):
        half, px = at // 2, at % 2
        for pz in range(zs):
            owner = ((me[0] ^ pz) * 2) + (me[1] ^ px)
            out.append(
                pltpu.make_async_copy(
                    buffer.at[pz, :, pl.ds(*first)],
                    scratch.at[half, pl.ds(owner * rows, rows), :],
                    sems.at[at, pz],
                )
            )
    return out


def emit_copies(me, staged, buffers, sems):
    zs, rows, _ = buffers[0].shape
    out = []
    for px, buffer in enumerate(buffers):
        for pz in range(zs):
            owner = ((me[0] ^ pz) * 2) + (me[1] ^ px)
            out.append(
                pltpu.make_async_copy(
                    staged.at[pl.ds(owner * rows, rows), :], buffer.at[pz], sems.at[px, pz]
                )
            )
    return out


def run(copies):
    for copy in copies:
        copy.start()
    for copy in copies:
        copy.wait()


def norm_in(x_ref, gain_ref, n_ref):
    x = x_ref[...].astype(F32)
    rstd = lax.rsqrt(jnp.mean(x * x, axis=1, keepdims=True) + EPSILON)
    n_ref[...] = (x * rstd * gain_ref[...].astype(F32)).astype(BF16)


def norm_first(x, gain):
    tokens, width = x.shape
    block = tokens // 4
    row = pl.BlockSpec((block, width), lambda i: (i, 0))
    return pl.pallas_call(
        norm_in,
        out_shape=jax.ShapeDtypeStruct((tokens, width), BF16),
        grid=(4,),
        in_specs=[row, pl.BlockSpec((1, width), lambda i: (0, 0))],
        out_specs=row,
        compiler_params=params(32),
        name="norm_first",
    )(x, gain)


def project_in(me_ref, n_ref, wa, wb, wc, wd, out_ref, w_scr, sems):
    @pl.when(pl.program_id(0) == 0)
    def _():
        run(fetch_copies(me_ref, (wa, wb, wc, wd), (0, w_scr.shape[2]), w_scr, sems))

    n = w_scr.shape[2]
    for half in range(2):
        out_ref[:, half * n : (half + 1) * n] = mm(n_ref[...], w_scr[half], NN).astype(BF16)


def project_qkv(me, normed, weights, columns):
    tokens, width = normed.shape
    block = tokens // 4
    zs = weights[0].shape[0]
    return pl.pallas_call(
        project_in,
        out_shape=jax.ShapeDtypeStruct((tokens, 2 * columns), BF16),
        grid=(4,),
        in_specs=[SCALARS, pl.BlockSpec((block, width), lambda i: (i, 0)), ANY, ANY, ANY, ANY],
        out_specs=pl.BlockSpec((block, 2 * columns), lambda i: (i, 0)),
        scratch_shapes=[
            pltpu.VMEM((2, width, columns), BF16),
            pltpu.SemaphoreType.DMA((4, zs)),
        ],
        compiler_params=params(32),
        name="project_qkv",
    )(me, normed, *weights)


def stack_heads(pair):
    lane = lax.broadcasted_iota(jnp.int32, pair.shape, 1)
    zero = jnp.zeros_like(pair)
    return jnp.concatenate(
        [jnp.where(lane < HEAD_DIM, pair, zero), jnp.where(lane < HEAD_DIM, zero, pair)], axis=0
    )


def masked_scores(length, key_rows, queries, first):
    raw = mm(key_rows, queries, NT)
    key_at = lax.broadcasted_iota(jnp.int32, raw.shape, 0)
    rows = raw.shape[1] // 2
    query_at = lax.broadcasted_iota(jnp.int32, raw.shape, 1)
    query_at = first + jnp.where(query_at >= rows, query_at - rows, query_at)
    return jnp.where((key_at <= query_at) & (key_at < length), raw, MASKED)


def attend_in(len_ref, q_ref, k_ref, v_ref, o_ref, lse_ref):
    tokens = q_ref.shape[0]
    rows = tokens // 4
    scale = HEAD_DIM ** (-0.5)
    length = len_ref[0]
    values_t = v_ref[...].T
    for at in range(4):
        first, last = at * rows, (at + 1) * rows
        queries = stack_heads(q_ref[first:last] * jnp.asarray(scale, BF16))
        scores = masked_scores(length, k_ref[:last], queries, first)
        peak = jnp.max(scores, axis=0, keepdims=True)
        expo = jnp.exp(scores - peak)
        denom = jnp.sum(expo, axis=0, keepdims=True)
        probs = (expo * (1.0 / denom)).astype(BF16)
        both = mm(values_t[:, :last], probs, NN)
        joined = jnp.concatenate([both[:HEAD_DIM, :rows], both[HEAD_DIM:, rows:]], axis=0)
        o_ref[first:last] = joined.T.astype(BF16)
        lse_ref[0, at : at + 1] = peak + jnp.log(denom)


def attend(length, qkv, heads):
    tokens = qkv.shape[0]
    pairs = heads // 2
    per = qkv.shape[1] // (6 * PAIR)

    def spec(which):
        return pl.BlockSpec(
            (tokens, PAIR), lambda i: (0, (i // per) * 3 * per + which * per + i % per)
        )

    return pl.pallas_call(
        attend_in,
        out_shape=(
            jax.ShapeDtypeStruct((tokens, pairs * PAIR), BF16),
            jax.ShapeDtypeStruct((pairs, 4, tokens // 2), F32),
        ),
        grid=(pairs,),
        in_specs=[SCALARS, spec(0), spec(1), spec(2)],
        out_specs=(
            pl.BlockSpec((tokens, PAIR), lambda i: (0, i)),
            pl.BlockSpec((1, 4, tokens // 2), lambda i: (i, 0, 0)),
        ),
        compiler_params=params(48),
        name="attend",
    )(length, qkv, qkv, qkv)


def project_out_in(me_ref, a_ref, wa, wb, wc, wd, out_ref, w_scr, sems):
    n = w_scr.shape[2]
    first = wa.shape[2] - n

    @pl.when(pl.program_id(0) == 0)
    def _():
        run(fetch_copies(me_ref, (wa, wb, wc, wd), (first, n), w_scr, sems))

    total = mm(a_ref[:, :n], w_scr[0], NT) + mm(a_ref[:, n:], w_scr[1], NT)
    out_ref[...] = total.astype(BF16)


def project_out(me, attended, weights):
    tokens, heads_wide = attended.shape
    zs, rows, _ = weights[0].shape
    width = zs * 2 * rows
    n = heads_wide // 2
    block = tokens // 4
    return pl.pallas_call(
        project_out_in,
        out_shape=jax.ShapeDtypeStruct((tokens, width), BF16),
        grid=(4,),
        in_specs=[SCALARS, pl.BlockSpec((block, 2 * n), lambda i: (i, 0)), ANY, ANY, ANY, ANY],
        out_specs=pl.BlockSpec((block, width), lambda i: (i, 0)),
        scratch_shapes=[pltpu.VMEM((2, width, n), BF16), pltpu.SemaphoreType.DMA((4, zs))],
        compiler_params=params(32),
        name="project_out",
    )(me, attended, *weights)


def norm_second_in(x_ref, own_ref, recv_ref, gain_ref, h_ref, n_ref):
    hidden = x_ref[...].astype(F32) + (own_ref[...].astype(F32) + recv_ref[...].astype(F32))
    h_ref[...] = hidden
    rstd = lax.rsqrt(jnp.mean(hidden * hidden, axis=1, keepdims=True) + EPSILON)
    n_ref[...] = (hidden * rstd * gain_ref[...].astype(F32)).astype(BF16)


def norm_second(x, own, recv, gain):
    tokens, width = x.shape
    row = pl.BlockSpec((tokens // 4, width), lambda i: (i, 0))
    return pl.pallas_call(
        norm_second_in,
        out_shape=(
            jax.ShapeDtypeStruct((tokens, width), F32),
            jax.ShapeDtypeStruct((tokens, width), BF16),
        ),
        grid=(4,),
        in_specs=[row, row, row, pl.BlockSpec((1, width), lambda i: (0, 0))],
        out_specs=(row, row),
        compiler_params=params(40),
        name="norm_second",
    )(x, own, recv, gain)


def mlp_in(first, me_ref, n_ref, m_ref, wa, wb, *refs):
    if first:
        mixed_ref, back_ref, g0, g1 = refs[:4]
        w_scr, grads, staged, sems, out_sems = refs[4:]
    else:
        mixed_acc, back_acc, mixed_ref, back_ref, g0, g1 = refs[:6]
        w_scr, grads, staged, sems, out_sems = refs[6:]
    step = pl.program_id(0)
    n = w_scr.shape[2] // 3

    @pl.when(step == 0)
    def _():
        run(fetch_copies(me_ref, (wa, wb), (0, 3 * n), w_scr, sems))

    normed, grad_mixed = n_ref[...], m_ref[...]
    parts = []
    for lo in range(0, n, 256):
        cut = slice(lo, lo + 256)
        gate = mm(normed, w_scr[0, :, lo : lo + 256], NN)
        up = mm(normed, w_scr[0, :, n + lo : n + lo + 256], NN)
        grad_hidden = mm(grad_mixed, w_scr[0, :, 2 * n + lo : 2 * n + lo + 256], NN)
        sig = 0.5 * jnp.tanh(0.5 * gate) + 0.5
        act = gate * sig
        hidden = (act * up).astype(BF16)
        grad_gate = (grad_hidden * up * (sig * (1.0 + gate * (1.0 - sig)))).astype(BF16)
        grad_up = (grad_hidden * act).astype(BF16)
        parts.append((grad_gate, grad_up, hidden))
    gate_all = jnp.concatenate([p[0] for p in parts], axis=1)
    up_all = jnp.concatenate([p[1] for p in parts], axis=1)
    hidden_all = jnp.concatenate([p[2] for p in parts], axis=1)
    mixed = mm(hidden_all, w_scr[0, :, 2 * n :], NT)
    back = mm(gate_all, w_scr[0, :, :n], NT) + mm(up_all, w_scr[0, :, n : 2 * n], NT)
    if not first:
        mixed = mixed + mixed_acc[...]
        back = back + back_acc[...]
    mixed_ref[...] = mixed.astype(mixed_ref.dtype)
    back_ref[...] = back.astype(back_ref.dtype)
    new = (
        mm(normed, gate_all, TN),
        mm(normed, up_all, TN),
        mm(grad_mixed, hidden_all, TN),
    )

    @pl.when(step == 0)
    def _():
        for at in range(3):
            grads[:, at * n : (at + 1) * n] = new[at]

    @pl.when(step == pl.num_programs(0) - 1)
    def _():
        for at in range(3):
            cut = slice(at * n, (at + 1) * n)
            staged[:, cut] = (grads[:, cut] + new[at]).astype(BF16)
        run(emit_copies(me_ref, staged, (g0, g1), out_sems))


def mlp(me, normed, grad_mixed, wa, wb, accs):
    tokens, width = normed.shape
    zs, rows, n3 = wa.shape
    block = tokens // 2
    row = pl.BlockSpec((block, width), lambda i: (i, 0))
    first = accs is None
    kind = F32 if first else BF16
    extra = [] if first else [row, row]
    return pl.pallas_call(
        functools.partial(mlp_in, first),
        out_shape=(
            jax.ShapeDtypeStruct((tokens, width), kind),
            jax.ShapeDtypeStruct((tokens, width), kind),
            jax.ShapeDtypeStruct((zs, rows, n3), BF16),
            jax.ShapeDtypeStruct((zs, rows, n3), BF16),
        ),
        grid=(2,),
        in_specs=[SCALARS, row, row, ANY, ANY] + extra,
        out_specs=(row, row, ANY, ANY),
        scratch_shapes=[
            pltpu.VMEM((1, width, n3), BF16),
            pltpu.VMEM((width, n3), F32),
            pltpu.VMEM((width, n3), BF16),
            pltpu.SemaphoreType.DMA((2, zs)),
            pltpu.SemaphoreType.DMA((2, zs)),
        ],
        compiler_params=params(60),
        name="mlp",
    )(me, normed, grad_mixed, wa, wb, *(() if first else accs))


def norm_second_back_in(
    h_ref, own_ref, recv_ref, gm_ref, gain_ref, gh_ref, gb_ref, gg_ref
):
    hidden = h_ref[...]
    width = hidden.shape[1]
    rstd = lax.rsqrt(jnp.mean(hidden * hidden, axis=1, keepdims=True) + EPSILON)
    grad = own_ref[...].astype(F32) + recv_ref[...].astype(F32)
    weighted = grad * gain_ref[...].astype(F32)
    stat = jnp.sum(weighted * hidden, axis=1, keepdims=True)
    grad_h = (
        gm_ref[...].astype(F32)
        + rstd * weighted
        - hidden * (rstd * rstd * rstd * stat / width)
    )
    gh_ref[...] = grad_h
    gb_ref[...] = grad_h.astype(BF16)
    piece = jnp.sum(grad * hidden * rstd, axis=0, keepdims=True)

    @pl.when(pl.program_id(0) == 0)
    def _():
        gg_ref[...] = jnp.zeros_like(gg_ref)

    gg_ref[...] += piece


def norm_second_back(hidden, own, recv, grad_mixed, gain):
    tokens, width = hidden.shape
    row = pl.BlockSpec((tokens // 4, width), lambda i: (i, 0))
    one = pl.BlockSpec((1, width), lambda i: (0, 0))
    return pl.pallas_call(
        norm_second_back_in,
        out_shape=(
            jax.ShapeDtypeStruct((tokens, width), F32),
            jax.ShapeDtypeStruct((tokens, width), BF16),
            jax.ShapeDtypeStruct((1, width), F32),
        ),
        grid=(4,),
        in_specs=[row, row, row, row, one],
        out_specs=(row, row, one),
        compiler_params=params(40),
        name="norm_second_back",
    )(hidden, own, recv, grad_mixed, gain)


def out_back_in(me_ref, gb_ref, a_ref, wa, wb, wc, wd, ga_ref, g0, g1, g2, g3, *scratch):
    w_scr, grads, staged, sems, out_sems = scratch
    n = w_scr.shape[2]
    first = wa.shape[2] - n
    step = pl.program_id(0)

    @pl.when(step == 0)
    def _():
        run(fetch_copies(me_ref, (wa, wb, wc, wd), (first, n), w_scr, sems))

    for half in range(2):
        ga_ref[:, half * n : (half + 1) * n] = mm(gb_ref[...], w_scr[half], NN).astype(BF16)
    new = mm(gb_ref[...], a_ref[...], TN)

    @pl.when(step == 0)
    def _():
        grads[...] = new

    @pl.when(step == pl.num_programs(0) - 1)
    def _():
        total = (grads[...] + new).astype(BF16)
        staged[0] = total[:, :n]
        staged[1] = total[:, n:]
        run(
            emit_copies(me_ref, staged.at[0], (g0, g1), out_sems.at[0])
            + emit_copies(me_ref, staged.at[1], (g2, g3), out_sems.at[1])
        )


def out_back(me, grad_branch, attended, weights):
    tokens, width = grad_branch.shape
    heads_wide = attended.shape[1]
    zs, rows, _ = weights[0].shape
    n = heads_wide // 2
    block = tokens // 2
    piece = jax.ShapeDtypeStruct((zs, rows, n), BF16)
    return pl.pallas_call(
        out_back_in,
        out_shape=(jax.ShapeDtypeStruct((tokens, heads_wide), BF16),) + (piece,) * 4,
        grid=(2,),
        in_specs=[
            SCALARS,
            pl.BlockSpec((block, width), lambda i: (i, 0)),
            pl.BlockSpec((block, heads_wide), lambda i: (i, 0)),
            ANY,
            ANY,
            ANY,
            ANY,
        ],
        out_specs=(pl.BlockSpec((block, heads_wide), lambda i: (i, 0)),) + (ANY,) * 4,
        scratch_shapes=[
            pltpu.VMEM((2, width, n), BF16),
            pltpu.VMEM((width, heads_wide), F32),
            pltpu.VMEM((2, width, n), BF16),
            pltpu.SemaphoreType.DMA((4, zs)),
            pltpu.SemaphoreType.DMA((2, 2, zs)),
        ],
        compiler_params=params(40),
        name="out_back",
    )(me, grad_branch, attended, *weights)


def attend_back_in(len_ref, q_ref, k_ref, v_ref, g_ref, lse_ref, gq_ref, gk_ref, gv_ref, *scratch):
    gk_acc, gv_acc = scratch
    tokens = q_ref.shape[0]
    rows = tokens // 4
    scale = HEAD_DIM ** (-0.5)
    length = len_ref[0]
    keys_t = k_ref[...].T
    gk_acc[...] = jnp.zeros_like(gk_acc)
    gv_acc[...] = jnp.zeros_like(gv_acc)
    for at in range(4):
        first, last = at * rows, (at + 1) * rows
        queries = stack_heads(q_ref[first:last] * jnp.asarray(scale, BF16))
        grads = stack_heads(g_ref[first:last])
        scores = masked_scores(length, k_ref[:last], queries, first)
        probs = jnp.exp(scores - lse_ref[0, at : at + 1])
        grad_probs = mm(v_ref[:last], grads, NT)
        inner = jnp.sum(probs * grad_probs, axis=0, keepdims=True)
        grad_scores = (probs * (grad_probs - inner)).astype(BF16)
        both = mm(keys_t[:, :last], grad_scores, NN)
        joined = jnp.concatenate([both[:HEAD_DIM, :rows], both[HEAD_DIM:, rows:]], axis=0)
        gq_ref[first:last] = (joined.T * scale).astype(BF16)
        gk_acc[:last] += mm(grad_scores, queries, NN)
        gv_acc[:last] += mm(probs.astype(BF16), grads, NN)
    gk_ref[...] = gk_acc[...].astype(BF16)
    gv_ref[...] = gv_acc[...].astype(BF16)


def attend_back(length, qkv, grad_attended, lse):
    tokens = qkv.shape[0]
    pairs = lse.shape[0]
    per = qkv.shape[1] // (6 * PAIR)

    def spec(which):
        return pl.BlockSpec(
            (tokens, PAIR), lambda i: (0, (i // per) * 3 * per + which * per + i % per)
        )

    own = pl.BlockSpec((tokens, PAIR), lambda i: (0, i))
    shape = jax.ShapeDtypeStruct((tokens, pairs * PAIR), BF16)
    return pl.pallas_call(
        attend_back_in,
        out_shape=(shape, shape, shape),
        grid=(pairs,),
        in_specs=[
            SCALARS,
            spec(0),
            spec(1),
            spec(2),
            own,
            pl.BlockSpec((1, 4, tokens // 2), lambda i: (i, 0, 0)),
        ],
        out_specs=(own, own, own),
        scratch_shapes=[pltpu.VMEM((tokens, PAIR), F32), pltpu.VMEM((tokens, PAIR), F32)],
        compiler_params=params(56),
        name="attend_back",
    )(length, qkv, qkv, qkv, grad_attended, lse)


def qkv_back_in(
    me_ref, gq_ref, gk_ref, gv_ref, n_ref, wa, wb, wc, wd, back_ref, g0, g1, g2, g3, *scratch
):
    w_scr, grads, staged, sems, out_sems = scratch
    columns = w_scr.shape[2]
    n = columns // 3
    step = pl.program_id(0)

    @pl.when(step == 0)
    def _():
        run(fetch_copies(me_ref, (wa, wb, wc, wd), (0, columns), w_scr, sems))

    total = None
    for half in range(2):
        cut = slice(half * n, (half + 1) * n)
        grad = jnp.concatenate([gq_ref[:, cut], gk_ref[:, cut], gv_ref[:, cut]], axis=1)
        piece = mm(grad, w_scr[half], NT)
        total = piece if total is None else total + piece
        new = mm(n_ref[...], grad, TN)

        @pl.when(step == 0)
        def _():
            grads[half] = new

        @pl.when(step == pl.num_programs(0) - 1)
        def _():
            staged[half] = (grads[half] + new).astype(BF16)

    back_ref[...] = total.astype(BF16)

    @pl.when(step == pl.num_programs(0) - 1)
    def _():
        run(
            emit_copies(me_ref, staged.at[0], (g0, g1), out_sems.at[0])
            + emit_copies(me_ref, staged.at[1], (g2, g3), out_sems.at[1])
        )


def qkv_back(me, grads, normed, weights, columns):
    tokens, width = normed.shape
    zs, rows, _ = weights[0].shape
    block = tokens // 2
    heads_wide = grads[0].shape[1]
    piece = jax.ShapeDtypeStruct((zs, rows, columns), BF16)
    grad_spec = pl.BlockSpec((block, heads_wide), lambda i: (i, 0))
    return pl.pallas_call(
        qkv_back_in,
        out_shape=(jax.ShapeDtypeStruct((tokens, width), BF16),) + (piece,) * 4,
        grid=(2,),
        in_specs=[
            SCALARS,
            grad_spec,
            grad_spec,
            grad_spec,
            pl.BlockSpec((block, width), lambda i: (i, 0)),
            ANY,
            ANY,
            ANY,
            ANY,
        ],
        out_specs=(pl.BlockSpec((block, width), lambda i: (i, 0)),) + (ANY,) * 4,
        scratch_shapes=[
            pltpu.VMEM((2, width, columns), BF16),
            pltpu.VMEM((2, width, columns), F32),
            pltpu.VMEM((2, width, columns), BF16),
            pltpu.SemaphoreType.DMA((4, zs)),
            pltpu.SemaphoreType.DMA((2, 2, zs)),
        ],
        compiler_params=params(48),
        name="qkv_back",
    )(me, *grads, normed, *weights)


def norm_first_back_in(x_ref, own_ref, recv_ref, gh_ref, gain_ref, gx_ref, gg_ref):
    x = x_ref[...].astype(F32)
    width = x.shape[1]
    rstd = lax.rsqrt(jnp.mean(x * x, axis=1, keepdims=True) + EPSILON)
    grad = own_ref[...].astype(F32) + recv_ref[...].astype(F32)
    weighted = grad * gain_ref[...].astype(F32)
    stat = jnp.sum(weighted * x, axis=1, keepdims=True)
    gx = gh_ref[...] + rstd * weighted - x * (rstd * rstd * rstd * stat / width)
    gx_ref[...] = gx.astype(BF16)

    @pl.when(pl.program_id(0) == 0)
    def _():
        gg_ref[...] = jnp.zeros_like(gg_ref)

    gg_ref[...] += jnp.sum(grad * x * rstd, axis=0, keepdims=True)


def norm_first_back(x, own, recv, grad_h, gain):
    tokens, width = x.shape
    row = pl.BlockSpec((tokens // 2, width), lambda i: (i, 0))
    one = pl.BlockSpec((1, width), lambda i: (0, 0))
    return pl.pallas_call(
        norm_first_back_in,
        out_shape=(
            jax.ShapeDtypeStruct((tokens, width), BF16),
            jax.ShapeDtypeStruct((1, width), F32),
        ),
        grid=(2,),
        in_specs=[row, row, row, row, one],
        out_specs=(row, one),
        compiler_params=params(40),
        name="norm_first_back",
    )(x, own, recv, grad_h, gain)


def shards(
    patches,
    w_query,
    w_key,
    w_value,
    w_out,
    w_gate,
    w_up,
    w_down,
    gain_attn,
    gain_mlp,
    lengths,
    cotangent,
):
    slab = patches.shape[1]
    rows_axis, cols_axis = lax.axis_size("row"), lax.axis_size("col")
    width = slab * cols_axis
    micro = lengths.shape[0]
    seq = patches.shape[0] // micro
    zs = rows_axis // 2
    row, col = lax.axis_index("row"), lax.axis_index("col")
    z, x, y, c = row // 2, row % 2, col // 2, col % 2
    me = jnp.stack([z, x, y, c]).astype(jnp.int32)
    heads_here = w_query.shape[1]
    columns = 3 * heads_here

    def swap(value, axis, bit):
        size = lax.axis_size(axis)
        return lax.ppermute(value, axis, [(i, i ^ bit) for i in range(size)])

    def gather(shard):
        near = jnp.stack([shard] + [swap(shard, "row", 2 * k) for k in range(1, zs)])
        beside = swap(near, "row", 1)
        across = swap(near, "col", 2)
        return near, beside, across, swap(across, "row", 1)

    def reduce_back(g00, g01, g10, g11):
        far = swap(g11, "row", 1)
        side = swap(g01, "row", 1)
        over = swap((g10.astype(F32) + far.astype(F32)).astype(BF16), "col", 2)

        def part(k):
            return g00[k].astype(F32) + (side[k].astype(F32) + over[k].astype(F32))

        total = part(0)
        for k in range(1, zs):
            total = total + swap(part(k).astype(BF16), "row", 2 * k).astype(F32)
        return total

    def pick(flag, one, other):
        return jnp.where(flag == 0, one, other)

    def spread(value):
        both = value.reshape(micro, seq, slab)
        mine = lax.dynamic_index_in_dim(both, y, 0, keepdims=False)
        theirs = lax.dynamic_index_in_dim(both, 1 - y, 0, keepdims=False)
        theirs = swap(theirs, "col", 2)
        pair = jnp.stack([mine, theirs])
        other = swap(pair, "col", 1)
        blocks = [
            pick(
                y ^ yy,
                pick(c ^ cc, pair[0], other[0]),
                pick(c ^ cc, pair[1], other[1]),
            )
            for yy in range(2)
            for cc in range(2)
        ]
        return jnp.concatenate(blocks, axis=1)

    def unspread(value):
        half = seq // 2
        quad = value.reshape(half, 2, 2, slab)
        stay = pick(c, quad[:, :, 0], quad[:, :, 1])
        leave = pick(c, quad[:, :, 1], quad[:, :, 0])
        come = swap(leave, "col", 1)
        whole = jnp.concatenate([pick(c, stay, come), pick(c, come, stay)], axis=0)
        keep = pick(y, whole[:, 0], whole[:, 1])
        send = pick(y, whole[:, 1], whole[:, 0])
        got = swap(send, "col", 2)
        return jnp.concatenate([pick(y, keep, got), pick(y, got, keep)], axis=0)

    inner = w_gate.shape[1]
    padded = -(-inner // 256) * 256
    pad = ((0, 0), (0, padded - inner))
    attn_shard = jnp.concatenate([w_query, w_key, w_value, w_out.T], axis=1)
    mlp_shard = jnp.concatenate(
        [jnp.pad(w_gate, pad), jnp.pad(w_up, pad), jnp.pad(w_down.T, pad)], axis=1
    )
    gains = lax.all_gather(jnp.stack([gain_attn, gain_mlp]), "row", axis=1, tiled=True)
    attn_gain, mlp_gain = gains[0:1], gains[1:2]

    x_all = spread(patches)
    attn_w = gather(attn_shard)
    mlp_w = gather(mlp_shard)

    length = lax.dynamic_slice_in_dim(lengths, y, 1)
    grad_mixed = spread(cotangent)
    grad_mixed = jnp.where(
        lax.iota(jnp.int32, seq)[:, None] < length, grad_mixed, jnp.zeros((), BF16)
    )

    normed_one = norm_first(x_all, attn_gain)
    qkv = project_qkv(me, normed_one, attn_w, columns)
    attended, lse = attend(length, qkv, 2 * heads_here // HEAD_DIM)
    branch = project_out(me, attended, attn_w)
    hidden, normed_two = norm_second(x_all, branch, swap(branch, "col", 1), mlp_gain)

    first = mlp(me, normed_two, grad_mixed, mlp_w[0], mlp_w[1], None)
    second = mlp(me, normed_two, grad_mixed, mlp_w[2], mlp_w[3], first[:2])
    mixed, back_two = second[:2]
    grad_h, grad_branch, mlp_gain_grad = norm_second_back(
        hidden, back_two, swap(back_two, "col", 1), grad_mixed, mlp_gain
    )
    mlp_grad = reduce_back(first[2], first[3], second[2], second[3])

    half = seq // 2

    def own_half(value):
        return lax.dynamic_slice_in_dim(value, c * half, half)

    def other_half(value):
        return lax.dynamic_slice_in_dim(value, (1 - c) * half, half)

    total = own_half(hidden) + (
        own_half(mixed).astype(F32) + swap(other_half(mixed), "col", 1).astype(F32)
    )
    valid = (lax.iota(jnp.int32, half) + c * half)[:, None] < length
    output = unspread(jnp.where(valid, total, 0.0).astype(BF16))

    back = out_back(me, grad_branch, attended, attn_w)
    out_grad = reduce_back(*back[1:])
    grads = attend_back(length, qkv, back[0], lse)
    back_one, *pieces = qkv_back(me, grads, normed_one, attn_w, columns)
    qkv_grad = reduce_back(*pieces)
    grad_x, attn_gain_grad = norm_first_back(
        own_half(x_all), own_half(back_one), swap(other_half(back_one), "col", 1),
        own_half(grad_h), attn_gain,
    )
    grad_patches = unspread(grad_x).astype(F32)

    gain_grads = lax.psum(
        jnp.concatenate([attn_gain_grad, 0.5 * mlp_gain_grad], axis=0), ("row", "col")
    )
    own_rows = width // rows_axis
    gain_grads = lax.dynamic_slice_in_dim(gain_grads, row * own_rows, own_rows, axis=1)

    return (
        output,
        grad_patches,
        qkv_grad[:, :heads_here],
        qkv_grad[:, heads_here : 2 * heads_here],
        qkv_grad[:, 2 * heads_here :],
        out_grad.T,
        mlp_grad[:, :inner],
        mlp_grad[:, padded : padded + inner],
        mlp_grad[:, 2 * padded : 2 * padded + inner].T,
        gain_grads[0],
        gain_grads[1],
    )


def solution(mesh):
    placed = (
        P("row", "col"),
        P("row", "col"),
        P("row", "col"),
        P("row", "col"),
        P("col", "row"),
        P("row", "col"),
        P("row", "col"),
        P("col", "row"),
        P("row"),
        P("row"),
        P("row"),
        P("row", "col"),
    )
    return jax.shard_map(
        shards,
        mesh=mesh,
        in_specs=placed,
        out_specs=(
            P("row", "col"),
            P("row", "col"),
            P("row", "col"),
            P("row", "col"),
            P("row", "col"),
            P("col", "row"),
            P("row", "col"),
            P("row", "col"),
            P("col", "row"),
            P("row"),
            P("row"),
        ),
        check_vma=False,
    )
```

time: 1460 us -> 613 us (0.42)
  waiting for transfers between devices: 837 us -> 204 us
  matrix products: 278 us -> 0 us
  Pallas kernels: 0 us -> 133 us
  blocking collectives: 209 us -> 135 us
  starting transfers between devices: 2.65 us -> 54.6 us
  other arithmetic: 71 us -> 37.3 us
  between operations: 17.7 us -> 1.59 us
    reduce_scatter x15 -> x0, waiting for transfers between devices: 653 us -> none  [the longest x8 165 us: reduce_cols(): lax.psum_scatter(partial_value, 'col', scatter_dimension=1, tiled=True)]
    dot_general x154 -> x0, matrix products: 278 us -> none  [the longest x62 117 us: times_trans(): lax.dot_general(left, right, (((1,), (1,)), ((), ())), preferred_element_...]
    ppermute x0 -> x42, waiting for transfers between devices: none -> 204 us  [swap(): return lax.ppermute(value, axis, [(i, i ^ bit) for i in range(size)])]
    all_gather x11 -> x0, waiting for transfers between devices: 180 us -> none  [the longest x8 102 us: to_full(): return lax.all_gather(values_own, 'col', axis=1, tiled=True)]
    pallas_call x0 -> x12, Pallas kernels: none -> 133 us  [the longest x2 51.9 us: mlp(): pl.pallas_call(functools.partial(mlp_in, first), out_shape=(jax.ShapeDtyp...]
    all_gather x6 -> x1, blocking collectives: 163 us -> 46.6 us  [shards(): lax.all_gather(jnp.stack([gain_attn, gain_mlp]), 'row', axis=1, tiled=True)]
    psum x4 -> x1, blocking collectives: 24.9 us -> 88.5 us  [shards(): lax.psum(jnp.concatenate([attn_gain_grad, 0.5 * mlp_gain_grad], axis=0),...]
    ppermute x0 -> x42, starting transfers between devices: none -> 54.6 us  [swap(): return lax.ppermute(value, axis, [(i, i ^ bit) for i in range(size)])]
  transfers between devices with their start and end apart: 26 -> 42, of which waited for: 19 -> 21; matrix products, arithmetic and copies ran while one was open for 22% -> 9% of each run, Pallas kernels for 0% -> 18%
where the time goes in v1:
time: 613 us; the launch traced here: 605 us
  waiting for transfers between devices  204 us (33%)
  blocking collectives  135 us (22%)
  Pallas kernels  133 us (22%)
  starting transfers between devices  54.6 us (9%)
  local copies, waits for them, and re-layouts  39.7 us (6%)
  other arithmetic  37.3 us (6%)
    ppermute x42, waiting for transfers between devices, swap(): return lax.ppermute(value, axis, [(i, i ^ bit) for i in range(size)])  204 us
    psum x1, blocking collectives, shards(): lax.psum(jnp.concatenate([attn_gain_grad, 0.5 * mlp_gain_grad], axis=0),...  88.5 us
    ppermute x42, starting transfers between devices, swap(): return lax.ppermute(value, axis, [(i, i ^ bit) for i in range(size)])  54.6 us
    pallas_call x2, Pallas kernels, mlp(): pl.pallas_call(functools.partial(mlp_in, first), out_shape=(jax.ShapeDtyp...  51.9 us
    all_gather x1, blocking collectives, shards(): lax.all_gather(jnp.stack([gain_attn, gain_mlp]), 'row', axis=1, tiled=True)  46.6 us
    unnamed x108, local copies, waits for them, and re-layouts  23.7 us
    pallas_call x1, Pallas kernels, attend_back(): pl.pallas_call(attend_back_in, out_shape=(shape, shape, shape), grid=(pai...  20.8 us
    pallas_call x1, Pallas kernels, qkv_back(): pl.pallas_call(qkv_back_in, out_shape=(jax.ShapeDtypeStruct((tokens, widt...  16.6 us
  transfers between devices with their start and end apart: 42, of which 21 were waited for; matrix products, arithmetic and copies ran while one was open for 9% of the time, Pallas kernels for 18%

profile of v1, /device:TPU:0, one launch (start us, length us, event | category | flops | bytes accessed | tf_op | source)
XLA Modules:
  0.0 604.9 jit_solution(2696737292899318236)
XLA Ops:
  3.9 4.1 collective-permute-start.12
  9.6 26.1 %collective-permute-done.12 = bf16[128,2304]{1,0:T(8,128)(2,1)S(1)} collective-permute-done((bf16[128,2304]{1,0:T(8,128)(2,1)S(1)}, bf16[128,2304]{1,0:T(8,128)(2,1)S(1)}, u32[]{:S(2)}, u32[]{:S(2)}) %collective-permute-start.12) | collective-permute-done | bytes 589856 | tf_op jit(solution)/shard_map/ppermute | solution.py:629
  35.7 12.1 %collective-permute-done.13 = bf16[128,2304]{1,0:T(8,128)(2,1)S(1)} collective-permute-done((bf16[128,2304]{1,0:T(8,128)(2,1)S(1)}, bf16[128,2304]{1,0:T(8,128)(2,1)S(1)}, u32[]{:S(2)}, u32[]{:S(2)}) %collective-permute-start.13) | collective-permute-done | bytes 589856 | tf_op jit(solution)/shard_map/ppermute | solution.py:629
  51.3 14.1 %collective-permute-start.3 = (bf16[128,1024]{1,0:T(8,128)(2,1)S(1)}, bf16[128,1024]{1,0:T(8,128)(2,1)S(1)}, u32[]{:S(2)}, u32[]{:S(2)}) collective-permute-start(bf16[128,1024]{1,0:T(8,128)(2,1)S(1)} %get-tuple-element.135), channel_id=1, source_target_pairs={{0,16},{4,20},{8,24},{12,28},{16,0},{20,4},{24,8},{28,12},{1,17},{... | collective-permute-start | bytes 786440 | tf_op jit(solution)/shard_map/ppermute | solution.py:629
  67.6 11.1 %collective-permute-done.3 = bf16[128,1024]{1,0:T(8,128)(2,1)S(1)} collective-permute-done((bf16[128,1024]{1,0:T(8,128)(2,1)S(1)}, bf16[128,1024]{1,0:T(8,128)(2,1)S(1)}, u32[]{:S(2)}, u32[]{:S(2)}) %collective-permute-start.3) | collective-permute-done | bytes 262176 | tf_op jit(solution)/shard_map/ppermute | solution.py:629
  78.7 5.3 collective-permute-done.2
  84.8 30.4 %collective-permute-done = bf16[1024,256]{1,0:T(8,128)(2,1)S(1)} collective-permute-done((bf16[1024,256]{1,0:T(8,128)(2,1)S(1)}, bf16[1024,256]{1,0:T(8,128)(2,1)S(1)}, u32[]{:S(2)}, u32[]{:S(2)}) %collective-permute-start) | collective-permute-done | bytes 524320 | tf_op jit(solution)/shard_map/ppermute | solution.py:629
  117.8 17.8 %collective-permute-done.6.wc = bf16[4,128,1024]{2,1,0:T(8,128)(2,1)S(1)} collective-permute-done((bf16[4,128,1024]{2,1,0:T(8,128)(2,1)S(1)}, bf16[4,128,1024]{2,1,0:T(8,128)(2,1)S(1)}, u32[]{:S(2)}, u32[]{:S(2)}) %collective-permute-start.6) | collective-permute-done | bytes 1048608 | tf_op jit(solution)/shard_map/ppermute | solution.py:629
  140.2 46.6 %all_gather.3 = bf16[2,1024]{1,0:T(2,128)(2,1)S(1)} all-gather(bf16[2,128]{1,0:T(2,128)(2,1)S(1)} %pad_maximum_fusion.10), channel_id=1, replica_groups=mesh['row'=8,'col'=4] {'row'}, dimensions={1}, use_global_device_ids=true | all-gather | bytes 4608 | tf_op jit(solution)/shard_map/all_gather | solution.py:690
  194.6 6.2 %project_qkv.1.q_ref.k_ref.v_ref = bf16[1024,1536]{1,0:T(8,128)(2,1)S(1)} custom-call(s32[4]{0:T(128)S(1)} %pad_add_fusion.me_ref, bf16[1024,1024]{1,0:T(8,128)(2,1)S(1)} %norm_first.1.n_ref, bf16[4,128,1024]{2,1,0:T(8,128)(2,1)S(1)} %copy-done.3, bf16[4,128,1024]{2,1,0:T(8,128)(2,1)S(1)} %copy-done.12, bf16[4,128,1024]{2,1,0:T(8,128)(2,1)S(1)} %copy-done.9, ...), custom_call_target="tpu_custom_call" | custom-call | tf_op jit(solution)/shard_map/project_qkv/pallas_call | solution.py:109
  202.2 13.4 %attend.1 = (bf16[1024,512]{1,0:T(8,128)(2,1)S(1)}, f32[4,4,512]{2,1,0:T(4,128)S(1)}) custom-call(s32[1]{0:T(128)} %dynamic_slice.40.len_ref, bf16[1024,1536]{1,0:T(8,128)(2,1)S(1)} %project_qkv.1.q_ref.k_ref.v_ref, bf16[1024,1536]{1,0:T(8,128)(2,1)S(1)} %project_qkv.1.q_ref.k_ref.v_ref, bf16[1024,1536]{1,0:T(8,128)(2,1)S(1)} %project_qkv.1.q_ref.k_ref.v_ref), custom_call_target="tpu_custom_call" | custom-call | tf_op jit(solution)/shard_map/attend/pallas_call | solution.py:171
  216.2 4.9 project_out.1.own_ref
  223.5 3.4 collective-permute-done.10
  230.4 3.5 norm_second.1
  237.3 4.2 collective-permute-done.16.wb
  241.5 25.1 %mlp.2 = (f32[1024,1024]{1,0:T(8,128)}, f32[1024,1024]{1,0:T(8,128)}, bf16[4,128,2304]{2,1,0:T(8,128)(2,1)}, bf16[4,128,2304]{2,1,0:T(8,128)(2,1)}) custom-call(s32[4]{0:T(128)} %copy-done.26, bf16[1024,1024]{1,0:T(8,128)(2,1)} %copy-done.16, bf16[1024,1024]{1,0:T(8,128)(2,1)} %maximum_select_fusion.m_ref.gm_ref, bf16[4,128,2304]{2,1,0:T(8,128)(2,1)} %pad_maximum_fusion.wa, ...), custom_call_target="tpu_custom_call" | custom-call | tf_op jit(solution)/shard_map/mlp/pallas_call | solution.py:306
  266.6 21.5 %collective-permute-done.15.wb = bf16[4,128,2304]{2,1,0:T(8,128)(2,1)} collective-permute-done((bf16[4,128,2304]{2,1,0:T(8,128)(2,1)}, bf16[4,128,2304]{2,1,0:T(8,128)(2,1)}, u32[]{:S(2)}, u32[]{:S(2)}) %collective-permute-start.15) | collective-permute-done | bytes 2359328 | tf_op jit(solution)/shard_map/ppermute | solution.py:629
  288.1 26.8 %mlp.3 = (bf16[1024,1024]{1,0:T(8,128)(2,1)}, bf16[1024,1024]{1,0:T(8,128)(2,1)}, bf16[4,128,2304]{2,1,0:T(8,128)(2,1)}, bf16[4,128,2304]{2,1,0:T(8,128)(2,1)}) custom-call(s32[4]{0:T(128)} %copy-done.26, bf16[1024,1024]{1,0:T(8,128)(2,1)} %copy-done.16, bf16[1024,1024]{1,0:T(8,128)(2,1)} %maximum_select_fusion.m_ref.gm_ref, ...), custom_call_target="tpu_custom_call" | custom-call | tf_op jit(solution)/shard_map/mlp/pallas_call | solution.py:306
  320.2 3.5 select_convert_fusion
  340.3 5.1 norm_second_back.1
  345.5 6.9 %out_back.1 = (bf16[1024,512]{1,0:T(8,128)(2,1)S(1)}, bf16[4,128,256]{2,1,0:T(8,128)(2,1)S(1)}, bf16[4,128,256]{2,1,0:T(8,128)(2,1)S(1)}, bf16[4,128,256]{2,1,0:T(8,128)(2,1)S(1)}, bf16[4,128,256]{2,1,0:T(8,128)(2,1)}) custom-call(s32[4]{0:T(128)S(1)} %copy-done.27, bf16[1024,1024]{1,0:T(8,128)(2,1)S(1)} %get-tuple-element.48.gb_ref, ...), custom_call_target="tpu_custom_call" | custom-call | tf_op jit(solution)/shard_map/out_back/pallas_call | solution.py:409
  355.0 20.8 %attend_back.1 = (bf16[1024,512]{1,0:T(8,128)(2,1)}, bf16[1024,512]{1,0:T(8,128)(2,1)}, bf16[1024,512]{1,0:T(8,128)(2,1)}) custom-call(s32[1]{0:T(128)} %dynamic_slice.40.len_ref, bf16[1024,1536]{1,0:T(8,128)(2,1)} %copy-done, bf16[1024,1536]{1,0:T(8,128)(2,1)} %copy-done, bf16[1024,1536]{1,0:T(8,128)(2,1)} %copy-done, bf16[1024,512]{1,0:T(8,128)(2,1)} %copy-done.21, ...), custom_call_target="tpu_custom_call" | custom-call | tf_op jit(solution)/shard_map/attend_back/pallas_call | solution.py:474
  378.2 16.6 %qkv_back.1 = (bf16[1024,1024]{1,0:T(8,128)(2,1)}, bf16[4,128,768]{2,1,0:T(8,128)(2,1)S(1)}, bf16[4,128,768]{2,1,0:T(8,128)(2,1)}, bf16[4,128,768]{2,1,0:T(8,128)(2,1)S(1)}, bf16[4,128,768]{2,1,0:T(8,128)(2,1)}) custom-call(s32[4]{0:T(128)S(1)} %copy-done.27, bf16[1024,512]{1,0:T(8,128)(2,1)S(1)} %copy-done.18, bf16[1024,512]{1,0:T(8,128)(2,1)S(1)} %copy-done.19, ...), custom_call_target="tpu_custom_call" | custom-call | tf_op jit(solution)/shard_map/qkv_back/pallas_call | solution.py:538
  394.9 3.3 constant_dynamic-slice_fusion.2
  414.0 3.6 add_convert_fusion
  421.3 3.3 collective-permute-done.25
  433.6 88.5 %psum.7 = f32[2,1024]{1,0:T(2,128)S(1)} all-reduce(f32[2,1024]{1,0:T(2,128)S(1)} %pad_maximum_fusion.9), channel_id=1, replica_groups=mesh['row'=8,'col'=4] {'row','col'}, use_global_device_ids=true, to_apply=%region_0.1 | all-reduce | flops 2048 | bytes 16384 | tf_op jit(solution)/shard_map/psum | solution.py:742
  527.9 5.5 collective-permute-done.27
  536.6 7.3 %collective-permute-done.28 = bf16[128,768]{1,0:T(8,128)(2,1)S(1)} collective-permute-done((bf16[128,768]{1,0:T(8,128)(2,1)S(1)}, bf16[128,768]{1,0:T(8,128)(2,1)S(1)}, u32[]{:S(2)}, u32[]{:S(2)}) %collective-permute-start.28) | collective-permute-done | bytes 196640 | tf_op jit(solution)/shard_map/ppermute | solution.py:629
  553.7 19.6 %collective-permute-done.39 = bf16[128,2304]{1,0:T(8,128)(2,1)S(1)} collective-permute-done((bf16[128,2304]{1,0:T(8,128)(2,1)S(1)}, bf16[128,2304]{1,0:T(8,128)(2,1)S(1)}, u32[]{:S(2)}, u32[]{:S(2)}) %collective-permute-start.39) | collective-permute-done | bytes 589856 | tf_op jit(solution)/shard_map/ppermute | solution.py:629
  573.4 3.7 collective-permute-done.41
  577.0 23.1 %collective-permute-done.40 = bf16[128,2304]{1,0:T(8,128)(2,1)S(1)} collective-permute-done((bf16[128,2304]{1,0:T(8,128)(2,1)S(1)}, bf16[128,2304]{1,0:T(8,128)(2,1)S(1)}, u32[]{:S(2)}, u32[]{:S(2)}) %collective-permute-start.40) | collective-permute-done | bytes 589856 | tf_op jit(solution)/shard_map/ppermute | solution.py:629
  (227 shorter events, 116.0 us)
Async XLA Ops:
  3.9 31.8 %collective-permute-start.12 = (bf16[128,2304]{1,0:T(8,128)(2,1)S(1)}, bf16[128,2304]{1,0:T(8,128)(2,1)S(1)}, u32[]{:S(2)}, u32[]{:S(2)}) collective-permute-start(bf16[128,2304]{1,0:T(8,128)(2,1)S(1)} %fusion.7), channel_id=1, source_target_pairs={{0,16},{4,20},{8,24},{12,28},{16,0},{20,4},{24,8},{28,12},{1,17},{... | collective-permute-start | bytes 1769480 | tf_op jit(solution)/shard_map/ppermute | solution.py:629
  8.0 27.7 %collective-permute-start.11 = (bf16[128,2304]{1,0:T(8,128)(2,1)S(1)}, bf16[128,2304]{1,0:T(8,128)(2,1)S(1)}, u32[]{:S(2)}, u32[]{:S(2)}) collective-permute-start(bf16[128,2304]{1,0:T(8,128)(2,1)S(1)} %fusion.7), channel_id=1, source_target_pairs={{0,8},{4,12},{8,0},{12,4},{16,24},{20,28},{24,16},{28,20},{1,9},{5... | collective-permute-start | bytes 1769480 | tf_op jit(solution)/shard_map/ppermute | solution.py:629
  9.6 38.2 %collective-permute-start.13 = (bf16[128,2304]{1,0:T(8,128)(2,1)S(1)}, bf16[128,2304]{1,0:T(8,128)(2,1)S(1)}, u32[]{:S(2)}, u32[]{:S(2)}) collective-permute-start(bf16[128,2304]{1,0:T(8,128)(2,1)S(1)} %fusion.7), channel_id=1, source_target_pairs={{0,24},{4,28},{8,16},{12,20},{16,8},{20,12},{24,0},{28,4},{1,25},{... | collective-permute-start | bytes 1769480 | tf_op jit(solution)/shard_map/ppermute | solution.py:629
  49.5 137.5 %collective-permute-start.14 = (bf16[4,128,2304]{2,1,0:T(8,128)(2,1)}, bf16[4,128,2304]{2,1,0:T(8,128)(2,1)}, u32[]{:S(2)}, u32[]{:S(2)}) collective-permute-start(bf16[4,128,2304]{2,1,0:T(8,128)(2,1)} %pad_maximum_fusion.wa), channel_id=1, source_target_pairs={{0,2},{1,3},{2,0},{3,1},{4,6},{5,7},{6,4},{7,5},{8,10},{9,11},{10,... | collective-permute-start | bytes 7077896 | tf_op jit(solution)/shard_map/ppermute | solution.py:629
  51.3 27.4 %collective-permute-start.3 = (bf16[128,1024]{1,0:T(8,128)(2,1)S(1)}, bf16[128,1024]{1,0:T(8,128)(2,1)S(1)}, u32[]{:S(2)}, u32[]{:S(2)}) collective-permute-start(bf16[128,1024]{1,0:T(8,128)(2,1)S(1)} %get-tuple-element.135), channel_id=1, source_target_pairs={{0,16},{4,20},{8,24},{12,28},{16,0},{20,4},{24,8},{28,12},{1,17},{... | collective-permute-start | bytes 786440 | tf_op jit(solution)/shard_map/ppermute | solution.py:629
  65.4 18.7 %collective-permute-start.2 = (bf16[128,1024]{1,0:T(8,128)(2,1)S(1)}, bf16[128,1024]{1,0:T(8,128)(2,1)S(1)}, u32[]{:S(2)}, u32[]{:S(2)}) collective-permute-start(bf16[128,1024]{1,0:T(8,128)(2,1)S(1)} %get-tuple-element.135), channel_id=1, source_target_pairs={{0,8},{4,12},{8,0},{12,4},{16,24},{20,28},{24,16},{28,20},{1,9},{5... | collective-permute-start | bytes 786440 | tf_op jit(solution)/shard_map/ppermute | solution.py:629
  65.4 18.7 %collective-permute-start.4 = (bf16[128,1024]{1,0:T(8,128)(2,1)S(1)}, bf16[128,1024]{1,0:T(8,128)(2,1)S(1)}, u32[]{:S(2)}, u32[]{:S(2)}) collective-permute-start(bf16[128,1024]{1,0:T(8,128)(2,1)S(1)} %get-tuple-element.135), channel_id=1, source_target_pairs={{0,24},{4,28},{8,16},{12,20},{16,8},{20,12},{24,0},{28,4},{1,25},{... | collective-permute-start | bytes 786440 | tf_op jit(solution)/shard_map/ppermute | solution.py:629
  67.0 48.1 %collective-permute-start = (bf16[1024,256]{1,0:T(8,128)(2,1)S(1)}, bf16[1024,256]{1,0:T(8,128)(2,1)S(1)}, u32[]{:S(2)}, u32[]{:S(2)}) collective-permute-start(bf16[1024,256]{1,0:T(8,128)(2,1)S(1)} %get-tuple-element.126), channel_id=1, source_target_pairs={{0,2},{1,3},{2,0},{3,1},{4,6},{5,7},{6,4},{7,5},{8,10},{9,11},{10,... | collective-permute-start | bytes 1572872 | tf_op jit(solution)/shard_map/ppermute | solution.py:629
  84.2 51.4 %collective-permute-start.6 = (bf16[4,128,1024]{2,1,0:T(8,128)(2,1)S(1)}, bf16[4,128,1024]{2,1,0:T(8,128)(2,1)S(1)}, u32[]{:S(2)}, u32[]{:S(2)}) collective-permute-start(bf16[4,128,1024]{2,1,0:T(8,128)(2,1)S(1)} %pad_maximum_fusion.3.wa), channel_id=1, source_target_pairs={{0,2},{1,3},{2,0},{3,1},{4,6},{5,7},{6,4},{7,5},{8,10},{9,11},{10,... | collective-permute-start | bytes 3145736 | tf_op jit(solution)/shard_map/ppermute | solution.py:629
  116.2 70.7 %collective-permute-start.1 = (bf16[2,1024,256]{2,1,0:T(8,128)(2,1)}, bf16[2,1024,256]{2,1,0:T(8,128)(2,1)}, u32[]{:S(2)}, u32[]{:S(2)}) collective-permute-start(bf16[2,1024,256]{2,1,0:T(8,128)(2,1)} %pad_maximum_fusion.2), channel_id=1, source_target_pairs={{0,1},{1,0},{2,3},{3,2},{4,5},{5,4},{6,7},{7,6},{8,9},{9,8},{10,11... | collective-permute-start | bytes 3145736 | tf_op jit(solution)/shard_map/ppermute | solution.py:629
  116.2 76.1 %collective-permute-start.5 = (bf16[4,128,1024]{2,1,0:T(8,128)(2,1)S(1)}, bf16[4,128,1024]{2,1,0:T(8,128)(2,1)S(1)}, u32[]{:S(2)}, u32[]{:S(2)}) collective-permute-start(bf16[4,128,1024]{2,1,0:T(8,128)(2,1)S(1)} %pad_maximum_fusion.3.wa), channel_id=1, source_target_pairs={{0,4},{4,0},{8,12},{12,8},{16,20},{20,16},{24,28},{28,24},{1,5},{5... | collective-permute-start | bytes 3145736 | tf_op jit(solution)/shard_map/ppermute | solution.py:629
  135.5 57.7 %collective-permute-start.7 = (bf16[4,128,1024]{2,1,0:T(8,128)(2,1)S(1)}, bf16[4,128,1024]{2,1,0:T(8,128)(2,1)}, u32[]{:S(2)}, u32[]{:S(2)}) collective-permute-start(bf16[4,128,1024]{2,1,0:T(8,128)(2,1)S(1)} %collective-permute-done.6.wc), channel_id=1, source_target_pairs={{0,4},{4,0},{8,12},{12,8},{16,20},{20,16},{24,28},{28,24},{1,5},{5... | collective-permute-start | bytes 3145736 | tf_op jit(solution)/shard_map/ppermute | solution.py:629
  138.1 83.1 %collective-permute-start.9 = (bf16[1024,256]{1,0:T(8,128)(2,1)}, bf16[1024,256]{1,0:T(8,128)(2,1)}, u32[]{:S(2)}, u32[]{:S(2)}) collective-permute-start(bf16[1024,256]{1,0:T(8,128)(2,1)} %get-tuple-element.124), channel_id=1, source_target_pairs={{0,2},{1,3},{2,0},{3,1},{4,6},{5,7},{6,4},{7,5},{8,10},{9,11},{10,... | collective-permute-start | bytes 1572872 | tf_op jit(solution)/shard_map/ppermute | solution.py:629
  186.9 54.6 %collective-permute-start.16 = (bf16[4,128,2304]{2,1,0:T(8,128)(2,1)}, bf16[4,128,2304]{2,1,0:T(8,128)(2,1)}, u32[]{:S(2)}, u32[]{:S(2)}) collective-permute-start(bf16[4,128,2304]{2,1,0:T(8,128)(2,1)} %pad_maximum_fusion.wa), channel_id=1, source_target_pairs={{0,4},{4,0},{8,12},{12,8},{16,20},{20,16},{24,28},{28,24},{1,5},{5... | collective-permute-start | bytes 7077896 | tf_op jit(solution)/shard_map/ppermute | solution.py:629
  187.0 101.1 %collective-permute-start.15 = (bf16[4,128,2304]{2,1,0:T(8,128)(2,1)}, bf16[4,128,2304]{2,1,0:T(8,128)(2,1)}, u32[]{:S(2)}, u32[]{:S(2)}) collective-permute-start(bf16[4,128,2304]{2,1,0:T(8,128)(2,1)} %collective-permute-done.14.wa), channel_id=1, source_target_pairs={{0,4},{4,0},{8,12},{12,8},{16,20},{20,16},{24,28},{28,24},{1,5},{5... | collective-permute-start | bytes 7077896 | tf_op jit(solution)/shard_map/ppermute | solution.py:629
  317.2 23.1 %collective-permute-start.20 = (bf16[1024,1024]{1,0:T(8,128)(2,1)}, bf16[1024,1024]{1,0:T(8,128)(2,1)}, u32[]{:S(2)}, u32[]{:S(2)}) collective-permute-start(bf16[1024,1024]{1,0:T(8,128)(2,1)} %get-tuple-element.47.own_ref), channel_id=1, source_target_pairs={{0,1},{1,0},{2,3},{3,2},{4,5},{5,4},{6,7},{7,6},{8,9},{9,8},{10,11... | collective-permute-start | bytes 6291464 | tf_op jit(solution)/shard_map/ppermute | solution.py:629
  334.4 78.1 %collective-permute-start.37 = (bf16[4,128,2304]{2,1,0:T(8,128)(2,1)}, bf16[4,128,2304]{2,1,0:T(8,128)(2,1)}, u32[]{:S(2)}, u32[]{:S(2)}) collective-permute-start(bf16[4,128,2304]{2,1,0:T(8,128)(2,1)} %get-tuple-element.68), channel_id=1, source_target_pairs={{0,4},{4,0},{8,12},{12,8},{16,20},{20,16},{24,28},{28,24},{1,5},{5... | collective-permute-start | bytes 7077896 | tf_op jit(solution)/shard_map/ppermute | solution.py:629
  338.7 62.8 %collective-permute-start.19 = (bf16[1024,256]{1,0:T(8,128)(2,1)}, bf16[1024,256]{1,0:T(8,128)(2,1)}, u32[]{:S(2)}, u32[]{:S(2)}) collective-permute-start(bf16[1024,256]{1,0:T(8,128)(2,1)} %select_bitcast_fusion.2), channel_id=1, source_target_pairs={{0,2},{1,3},{2,0},{3,1},{4,6},{5,7},{6,4},{7,5},{8,10},{9,11},{10,... | collective-permute-start | bytes 1572872 | tf_op jit(solution)/shard_map/ppermute | solution.py:629
  353.4 47.1 %collective-permute-start.31 = (bf16[4,128,256]{2,1,0:T(8,128)(2,1)}, bf16[4,128,256]{2,1,0:T(8,128)(2,1)}, u32[]{:S(2)}, u32[]{:S(2)}) collective-permute-start(bf16[4,128,256]{2,1,0:T(8,128)(2,1)} %get-tuple-element.64), channel_id=1, source_target_pairs={{0,4},{4,0},{8,12},{12,8},{16,20},{20,16},{24,28},{28,24},{1,5},{5... | collective-permute-start | bytes 786440 | tf_op jit(solution)/shard_map/ppermute | solution.py:629
  398.8 25.8 %collective-permute-start.25 = (bf16[4,128,768]{2,1,0:T(8,128)(2,1)}, bf16[4,128,768]{2,1,0:T(8,128)(2,1)}, u32[]{:S(2)}, u32[]{:S(2)}) collective-permute-start(bf16[4,128,768]{2,1,0:T(8,128)(2,1)} %get-tuple-element.60), channel_id=1, source_target_pairs={{0,4},{4,0},{8,12},{12,8},{16,20},{20,16},{24,28},{28,24},{1,5},{5... | collective-permute-start | bytes 2359304 | tf_op jit(solution)/shard_map/ppermute | solution.py:629
  400.5 27.4 %collective-permute-start.21 = (bf16[512,1024]{1,0:T(8,128)(2,1)}, bf16[512,1024]{1,0:T(8,128)(2,1)}, u32[]{:S(2)}, u32[]{:S(2)}) collective-permute-start(bf16[512,1024]{1,0:T(8,128)(2,1)} %get-tuple-element.99), channel_id=1, source_target_pairs={{0,1},{1,0},{2,3},{3,2},{4,5},{5,4},{6,7},{7,6},{8,9},{9,8},{10,11... | collective-permute-start | bytes 3145736 | tf_op jit(solution)/shard_map/ppermute | solution.py:629
  417.6 127.5 %collective-permute-start.36 = (bf16[4,128,2304]{2,1,0:T(8,128)(2,1)}, bf16[4,128,2304]{2,1,0:T(8,128)(2,1)}, u32[]{:S(2)}, u32[]{:S(2)}) collective-permute-start(bf16[4,128,2304]{2,1,0:T(8,128)(2,1)} %get-tuple-element.66), channel_id=1, source_target_pairs={{0,4},{4,0},{8,12},{12,8},{16,20},{20,16},{24,28},{28,24},{1,5},{5... | collective-permute-start | bytes 7077896 | tf_op jit(solution)/shard_map/ppermute | solution.py:629
  418.0 104.5 %collective-permute-start.24 = (bf16[4,128,768]{2,1,0:T(8,128)(2,1)}, bf16[4,128,768]{2,1,0:T(8,128)(2,1)}, u32[]{:S(2)}, u32[]{:S(2)}) collective-permute-start(bf16[4,128,768]{2,1,0:T(8,128)(2,1)} %get-tuple-element.58), channel_id=1, source_target_pairs={{0,4},{4,0},{8,12},{12,8},{16,20},{20,16},{24,28},{28,24},{1,5},{5... | collective-permute-start | bytes 2359304 | tf_op jit(solution)/shard_map/ppermute | solution.py:629
  419.7 125.3 %collective-permute-start.38 = (bf16[4,128,2304]{2,1,0:T(8,128)(2,1)}, bf16[4,128,2304]{2,1,0:T(8,128)(2,1)}, u32[]{:S(2)}, u32[]{:S(2)}) collective-permute-start(bf16[4,128,2304]{2,1,0:T(8,128)(2,1)} %add_convert_fusion), channel_id=1, source_target_pairs={{0,2},{1,3},{2,0},{3,1},{4,6},{5,7},{6,4},{7,5},{8,10},{9,11},{10,... | collective-permute-start | bytes 7077896 | tf_op jit(solution)/shard_map/ppermute | solution.py:629
  427.1 95.5 %collective-permute-start.26 = (bf16[4,128,768]{2,1,0:T(8,128)(2,1)}, bf16[4,128,768]{2,1,0:T(8,128)(2,1)}, u32[]{:S(2)}, u32[]{:S(2)}) collective-permute-start(bf16[4,128,768]{2,1,0:T(8,128)(2,1)} %add_convert_fusion.1), channel_id=1, source_target_pairs={{0,2},{1,3},{2,0},{3,1},{4,6},{5,7},{6,4},{7,5},{8,10},{9,11},{10,... | collective-permute-start | bytes 2359304 | tf_op jit(solution)/shard_map/ppermute | solution.py:629
  433.5 93.1 %collective-permute-start.22 = (bf16[512,2,256]{2,0,1:T(8,128)(2,1)S(1)}, bf16[512,2,256]{2,0,1:T(8,128)(2,1)S(1)}, u32[]{:S(2)}, u32[]{:S(2)}) collective-permute-start(bf16[512,2,256]{2,0,1:T(8,128)(2,1)S(1)} %select_bitcast_fusion.1), channel_id=1, source_target_pairs={{0,1},{1,0},{2,3},{3,2},{4,5},{5,4},{6,7},{7,6},{8,9},{9,8},{10,11... | collective-permute-start | bytes 1572872 | tf_op jit(solution)/shard_map/ppermute | solution.py:629
  524.7 11.9 %collective-permute-start.29 = (bf16[128,768]{1,0:T(8,128)(2,1)S(1)}, bf16[128,768]{1,0:T(8,128)(2,1)S(1)}, u32[]{:S(2)}, u32[]{:S(2)}) collective-permute-start(bf16[128,768]{1,0:T(8,128)(2,1)S(1)} %get-tuple-element.97), channel_id=1, source_target_pairs={{0,24},{4,28},{8,16},{12,20},{16,8},{20,12},{24,0},{28,4},{1,25},{... | collective-permute-start | bytes 589832 | tf_op jit(solution)/shard_map/ppermute | solution.py:629
  526.5 17.3 %collective-permute-start.28 = (bf16[128,768]{1,0:T(8,128)(2,1)S(1)}, bf16[128,768]{1,0:T(8,128)(2,1)S(1)}, u32[]{:S(2)}, u32[]{:S(2)}) collective-permute-start(bf16[128,768]{1,0:T(8,128)(2,1)S(1)} %get-tuple-element.98), channel_id=1, source_target_pairs={{0,16},{4,20},{8,24},{12,28},{16,0},{20,4},{24,8},{28,12},{1,17},{... | collective-permute-start | bytes 589832 | tf_op jit(solution)/shard_map/ppermute | solution.py:629
  533.4 18.6 %collective-permute-start.23 = (bf16[1024,256]{1,0:T(8,128)(2,1)S(1)}, bf16[1024,256]{1,0:T(8,128)(2,1)S(1)}, u32[]{:S(2)}, u32[]{:S(2)}) collective-permute-start(bf16[1024,256]{1,0:T(8,128)(2,1)S(1)} %select_bitcast_fusion), channel_id=1, source_target_pairs={{0,2},{1,3},{2,0},{3,1},{4,6},{5,7},{6,4},{7,5},{8,10},{9,11},{10,... | collective-permute-start | bytes 1572872 | tf_op jit(solution)/shard_map/ppermute | solution.py:629
  547.7 25.7 %collective-permute-start.39 = (bf16[128,2304]{1,0:T(8,128)(2,1)S(1)}, bf16[128,2304]{1,0:T(8,128)(2,1)S(1)}, u32[]{:S(2)}, u32[]{:S(2)}) collective-permute-start(bf16[128,2304]{1,0:T(8,128)(2,1)S(1)} %get-tuple-element.93), channel_id=1, source_target_pairs={{0,8},{4,12},{8,0},{12,4},{16,24},{20,28},{24,16},{28,20},{1,9},{5... | collective-permute-start | bytes 1769480 | tf_op jit(solution)/shard_map/ppermute | solution.py:629
  547.8 29.3 %collective-permute-start.41 = (bf16[128,2304]{1,0:T(8,128)(2,1)S(1)}, bf16[128,2304]{1,0:T(8,128)(2,1)S(1)}, u32[]{:S(2)}, u32[]{:S(2)}) collective-permute-start(bf16[128,2304]{1,0:T(8,128)(2,1)S(1)} %get-tuple-element.94), channel_id=1, source_target_pairs={{0,24},{4,28},{8,16},{12,20},{16,8},{20,12},{24,0},{28,4},{1,25},{... | collective-permute-start | bytes 1769480 | tf_op jit(solution)/shard_map/ppermute | solution.py:629
  550.1 50.0 %collective-permute-start.40 = (bf16[128,2304]{1,0:T(8,128)(2,1)S(1)}, bf16[128,2304]{1,0:T(8,128)(2,1)S(1)}, u32[]{:S(2)}, u32[]{:S(2)}) collective-permute-start(bf16[128,2304]{1,0:T(8,128)(2,1)S(1)} %get-tuple-element.95), channel_id=1, source_target_pairs={{0,16},{4,20},{8,24},{12,28},{16,0},{20,4},{24,8},{28,12},{1,17},{... | collective-permute-start | bytes 1769480 | tf_op jit(solution)/shard_map/ppermute | solution.py:629
  (58 other events, 681.1 us)
